TPU v7x, 512 devices: a whole 4x4x16 slice. The times are simulated.
512 devices in a mesh: mp: 64 (over x, z), replica: 8 (over y, core).
Axes of the slice: x: 4, y: 4, z: 16, core: 2. Of those that a mesh axis runs over, the one named last changes fastest.
Arguments:
- pooled_grads: bfloat16 [64, 8, 128, 64, 128], P('mp', 'replica'), may hold values from -0.119628906 to 0.119628906
- table: float32 [64, 512, 128], P('mp'), may hold values from -3 to 3
- state: float32 [64, 512], P('mp'), may hold values from 0.2 to 5
- tile_mult: bfloat16 [64, 8, 64, 128, 128], P('mp', 'replica'), may hold values from 0 to 3, as said below
- tile_rows: int32 [64, 8, 64], P('mp', 'replica'), may hold values from 0 to 3
Outputs:
- new_table: float32 [64, 512, 128], P('mp')
- new_state: float32 [64, 512], P('mp')
Inputs may be any that keep to these rules, and one draw needn't show every extreme that they name: tile_mult holds whole numbers.
All inputs are finite; a program needn't handle non-finite values.
Results may differ from a plain program's by a relative error of at most 0.0003.
Values may be sent and summed in bfloat16 or wider, within the bound.
No kernel may reach another device: no remote copies, remote signals or barrier semaphores. Data moves between devices by JAX's collectives and lax.ppermute only.
A program may use at most 64 MiB of HBM per device.

v0:
```python
import jax
import jax.numpy as jnp
from jax import lax
from jax.sharding import PartitionSpec as P

LEARN_RATE = 0.5
EPSILON = 1e-06


def adagrad(weights_in, accum_in, gradient):
    accum_out = accum_in + jnp.mean(gradient * gradient, axis=-1)
    weights_out = weights_in - LEARN_RATE * gradient / (jnp.sqrt(accum_out)[..., None] + EPSILON)
    return (weights_out, accum_out)


def on_device(pooled_grads, table, state, tile_mult, tile_rows):
    local_grads = pooled_grads[0, 0]
    width = local_grads.shape[-1]
    received = lax.all_to_all(local_grads, "mp", split_axis=1, concat_axis=0, tiled=True)
    counts_bf = tile_mult[0, 0]
    block_size = counts_bf.shape[-1]
    sample_blocks = received.reshape(-1, block_size, width)
    row_ids = tile_rows[0, 0]
    contrib = jnp.einsum(
        "tsr,tse->tre", counts_bf, sample_blocks, preferred_element_type=jnp.float32
    )
    weights_in = table[0]
    accum_in = state[0]
    row_count = weights_in.shape[0]
    row_blocks = row_count // block_size
    onehot = (row_ids[:, None] == jnp.arange(row_blocks, dtype=jnp.int32)[None, :]).astype(
        jnp.float32
    )
    partial_grad = jnp.einsum(
        "tb,tre->bre", onehot, contrib, precision=lax.Precision.HIGHEST
    ).reshape(row_count, width)
    total_grad = lax.psum(partial_grad, "replica")
    weights_out, accum_out = adagrad(weights_in, accum_in, total_grad)
    return (weights_out[None], accum_out[None])


def solution(mesh):
    placed = (
        P("mp", "replica", None, None, None),
        P("mp", None, None),
        P("mp", None),
        P("mp", "replica", None, None, None),
        P("mp", "replica", None),
    )
    return jax.shard_map(
        on_device,
        mesh=mesh,
        in_specs=placed,
        out_specs=(P("mp", None, None), P("mp", None)),
        check_vma=False,
    )
```

profile of v0, /device:TPU:1, one launch (start us, length us, event | category | flops | bytes accessed | tf_op | source)
XLA Modules:
  0.0 211.2 jit_solution(7404038184944069721)
XLA Ops:
  7.2 0.0 copy-start
  7.2 0.0 all-reduce.2.cloned.1.call-start
  7.2 3.1 %copy.16 = bf16[1,1,128,64,128]{4,2,3,1,0:T(8,128)(2,1)S(1)} copy(bf16[1,1,128,64,128]{4,3,2,1,0:T(8,128)(2,1)} %param.5) | data formatting | bytes 4194304 | tf_op args[0]
  10.3 113.6 %all_to_all.15 = bf16[128,64,128]{2,0,1:T(8,128)(2,1)S(1)} all-to-all(bf16[128,64,128]{2,0,1:T(8,128)(2,1)S(1)} %bitcast.26), channel_id=1, replica_groups=mesh['mp'=64,'replica'=8] {'mp'}, dimensions={1} | all-to-all | bytes 4194304 | tf_op jit(solution)/shard_map/all_to_all | solution.py:19
  123.9 0.0 copy-done
  123.9 0.0 copy-start.3
  123.9 0.9 fusion.2
  124.8 0.0 copy-done.3
  124.8 0.0 copy-start.2
  124.8 0.0 copy-start.1
  124.8 3.8 %fusion = f32[4,128,128]{2,0,1:T(4,128)S(1)} fusion(f32[64,128,128]{2,1,0:T(8,128)S(1)} %fusion.2, s32[64]{0:T(128)S(1)} %bitcast.30), kind=kOutput, calls=%fused_computation | convolution fusion | flops 50331904 | bytes 4456704 | tf_op jit(solution)/shard_map/tb,tre->bre/dot_general | solution.py:34
  128.6 0.7 copy.11
  129.3 0.0 all-reduce.2.cloned.1.call-update
  129.3 71.6 %all-reduce.2.cloned.1.call-done = f32[512,128]{1,0:T(8,128)} async-done(((f32[512,128]{1,0:T(8,128)}), f32[512,128]{1,0:T(8,128)}) %all-reduce.2.cloned.1.call-update) | async-done | bytes 262160 | tf_op jit(solution)/shard_map/psum | solution.py:37
  200.9 1.1 multiply_reduce_fusion
  202.0 0.0 copy-done.2
  202.0 0.6 add.26
  202.6 0.0 copy-done.1
  202.6 1.8 fusion.5
  (1 shorter events, 0.0 us)
Async XLA Ops:
  7.2 116.7 %copy-start = (bf16[1,1,64,128,128]{4,3,2,1,0:T(8,128)(2,1)S(1)}, bf16[1,1,64,128,128]{4,3,2,1,0:T(8,128)(2,1)}, u32[]{:S(2)}) copy-start(bf16[1,1,64,128,128]{4,3,2,1,0:T(8,128)(2,1)} %param.8) | copy-start | bytes 6291460
  7.2 193.7 %all-reduce.2.cloned.1.call-start = ((), (), s32[]{:S(2)}) async-start(), calls=%async_computation.1 | async-start | bytes 524288 | tf_op jit(solution)/shard_map/psum | solution.py:37
  123.9 0.9 copy-start.3
  124.8 77.2 %copy-start.2 = (f32[1,512]{1,0:T(1,128)S(1)}, f32[1,512]{1,0:T(1,128)}, u32[]{:S(2)}) copy-start(f32[1,512]{1,0:T(1,128)} %param.7) | copy-start | bytes 6148
  124.8 77.8 %copy-start.1 = (f32[1,512,128]{2,1,0:T(8,128)S(1)}, f32[1,512,128]{2,1,0:T(8,128)}, u32[]{:S(2)}) copy-start(f32[1,512,128]{2,1,0:T(8,128)} %param.6) | copy-start | bytes 786436
Sparse Core Ops, SparseCore 0:
  129.5 71.3 all-reduce.1
where the time goes:
time: 212 us; the launch traced here: 211 us
  blocking collectives  114 us (54%)
  waiting for transfers between devices  71.6 us (34%)
  between operations  14.1 us (7%)
  matrix products  4.67 us (2%)
  local copies, waits for them, and re-layouts  3.83 us (2%)
  other arithmetic  3.48 us (2%)
    all_to_all x1, blocking collectives, on_device(): lax.all_to_all(local_grads, 'mp', split_axis=1, concat_axis=0, tiled=True)  114 us
    psum x1, waiting for transfers between devices, on_device(): total_grad = lax.psum(partial_grad, 'replica')  71.6 us
  transfers between devices with their start and end apart: 1, of which 1 were waited for; matrix products, arithmetic and copies ran while one was open for 0% of the time, Pallas kernels for 0%

commit v1 on v0

v1 whole, which is shorter than its diff:
```python
import jax
import jax.numpy as jnp
from jax import lax
from jax.experimental import pallas as pl
from jax.experimental.pallas import tpu as pltpu
from jax.sharding import PartitionSpec as P

LEARN_RATE = 0.5
EPSILON = 1e-06


def accumulate_kernel(rows_ref, mult_ref, grads_ref, out_ref):
    tiles, block, _ = mult_ref.shape
    out_ref[...] = jnp.zeros(out_ref.shape, out_ref.dtype)

    def one_tile(t, carry):
        contrib = lax.dot_general(
            mult_ref[t], grads_ref[t], (((0,), (0,)), ((), ())), preferred_element_type=jnp.float32
        )
        out_ref[rows_ref[t]] += contrib
        return carry

    lax.fori_loop(0, tiles, one_tile, 0, unroll=8)


def accumulate(row_ids, mult, grads, row_blocks):
    _, block, width = grads.shape
    vmem = pl.BlockSpec(memory_space=pltpu.VMEM)
    return pl.pallas_call(
        accumulate_kernel,
        out_shape=jax.ShapeDtypeStruct((row_blocks, block, width), jnp.float32),
        in_specs=[pl.BlockSpec(memory_space=pltpu.SMEM), vmem, vmem],
        out_specs=vmem,
        name="accumulate",
    )(row_ids, mult, grads)


def adagrad(weights_in, accum_in, gradient):
    accum_out = accum_in + jnp.mean(gradient * gradient, axis=-1)
    weights_out = weights_in - LEARN_RATE * gradient / (jnp.sqrt(accum_out)[..., None] + EPSILON)
    return (weights_out, accum_out)


def on_device(pooled_grads, table, state, tile_mult, tile_rows):
    weights_in = table[0]
    accum_in = state[0]
    mult = tile_mult[0, 0]
    rows, width = weights_in.shape
    row_blocks = rows // mult.shape[-1]
    replicas = lax.axis_size("replica")

    by_table = jnp.transpose(pooled_grads[0, 0], (1, 0, 2))
    received = lax.all_to_all(by_table, "mp", split_axis=0, concat_axis=0, tiled=True)
    partial_grad = accumulate(tile_rows[0, 0], mult, received, row_blocks)

    shares = partial_grad.reshape(replicas, rows // replicas, width)
    shares = lax.all_to_all(shares, "replica", split_axis=0, concat_axis=0, tiled=True)
    own = jnp.sum(shares, axis=0)
    copies = jnp.broadcast_to(own[None], (replicas,) + own.shape)
    total_grad = lax.all_to_all(copies, "replica", split_axis=0, concat_axis=0, tiled=True)

    weights_out, accum_out = adagrad(weights_in, accum_in, total_grad.reshape(rows, width))
    return (weights_out[None], accum_out[None])


def solution(mesh):
    placed = (
        P("mp", "replica", None, None, None),
        P("mp", None, None),
        P("mp", None),
        P("mp", "replica", None, None, None),
        P("mp", "replica", None),
    )
    return jax.shard_map(
        on_device,
        mesh=mesh,
        in_specs=placed,
        out_specs=(P("mp", None, None), P("mp", None)),
        check_vma=False,
    )
```

time: 212 us -> 149 us (0.70)
  waiting for transfers between devices: 71.6 us -> 0 us
  blocking collectives: 114 us -> 139 us
  between operations: 14.1 us -> 0.66 us
  Pallas kernels: 0 us -> 5.15 us
  matrix products: 4.67 us -> 0 us
    psum x1 -> x0, waiting for transfers between devices: 71.6 us -> none  [on_device(): total_grad = lax.psum(partial_grad, 'replica')]
    all_to_all x1 -> x3, blocking collectives: 114 us -> 139 us  [the longest x1 114 us: on_device(): lax.all_to_all(by_table, 'mp', split_axis=0, concat_axis=0, tiled=True)]
    pallas_call x0 -> x1, Pallas kernels: none -> 5.15 us  [accumulate(): pl.pallas_call(accumulate_kernel, out_shape=jax.ShapeDtypeStruct((row_blo...]
    dot_general x2 -> x0, matrix products: 4.67 us -> none  [the longest x1 3.8 us: on_device(): jnp.einsum('tb,tre->bre', onehot, contrib, precision=lax.Precision.HIGHEST)]
  transfers between devices with their start and end apart: 1 -> 0, of which waited for: 1 -> 0; matrix products, arithmetic and copies ran while one was open for 0% -> 0% of each run, Pallas kernels for 0% -> 0%
where the time goes in v1:
time: 149 us
  blocking collectives  139 us (93%)
  Pallas kernels  5.15 us (3%)
  local copies, waits for them, and re-layouts  3.12 us (2%)
  other arithmetic  1.6 us (1%)
    all_to_all x1, blocking collectives, on_device(): lax.all_to_all(by_table, 'mp', split_axis=0, concat_axis=0, tiled=True)  114 us
    all_to_all x1, blocking collectives, on_device(): lax.all_to_all(shares, 'replica', split_axis=0, concat_axis=0, tiled=True)  14.9 us
    all_to_all x1, blocking collectives, on_device(): lax.all_to_all(copies, 'replica', split_axis=0, concat_axis=0, tiled=True)  9.91 us
    pallas_call x1, Pallas kernels, accumulate(): pl.pallas_call(accumulate_kernel, out_shape=jax.ShapeDtypeStruct((row_blo...  5.15 us

profile of v1, /device:TPU:1, one launch (start us, length us, event | category | flops | bytes accessed | tf_op | source)
XLA Modules:
  0.0 149.1 jit_solution(3818656373853117001)
XLA Ops:
  0.6 2.9 %copy.9 = bf16[1,1,128,64,128]{4,2,3,1,0:T(8,128)(2,1)S(1)} copy(bf16[1,1,128,64,128]{4,3,2,1,0:T(8,128)(2,1)} %param.5) | data formatting | bytes 4194304 | tf_op args[0]
  3.6 113.7 %all_to_all.15.grads_ref = bf16[64,128,128]{2,1,0:T(8,128)(2,1)} all-to-all(bf16[64,128,128]{2,1,0:T(8,128)(2,1)S(1)} %bitcast.14), channel_id=1, replica_groups=mesh['mp'=64,'replica'=8] {'mp'}, dimensions={0} | all-to-all | bytes 4194304 | tf_op jit(solution)/shard_map/all_to_all | solution.py:53
  117.3 5.1 %accumulate.1 = f32[4,128,128]{2,1,0:T(8,128)} custom-call(s32[64]{0:T(128)} %bitcast.19, bf16[64,128,128]{2,1,0:T(8,128)(2,1)} %bitcast.15, bf16[64,128,128]{2,1,0:T(8,128)(2,1)} %all_to_all.15.grads_ref), custom_call_target="tpu_custom_call" | custom-call | tf_op jit(solution)/shard_map/accumulate/pallas_call | solution.py:29
  122.4 0.0 copy-start.1
  122.4 0.0 copy-start
  122.4 14.9 %all_to_all.16 = f32[8,64,128]{2,1,0:T(8,128)S(1)} all-to-all(f32[8,64,128]{2,1,0:T(8,128)} %bitcast.17), channel_id=1, replica_groups=mesh['mp'=64,'replica'=8] {'replica'}, dimensions={0} | all-to-all | bytes 524288 | tf_op jit(solution)/shard_map/all_to_all | solution.py:57
  137.4 9.9 %all_to_all.17 = f32[8,64,128]{2,1,0:T(8,128)S(1)} all-to-all(f32[8,64,128]{2,1,0:T(8,128)S(1)} %broadcast_in_dim.2), channel_id=1, replica_groups=mesh['mp'=64,'replica'=8] {'replica'}, dimensions={0} | all-to-all | bytes 524288 | tf_op jit(solution)/shard_map/all_to_all | solution.py:60
  147.3 0.1 multiply_reduce_fusion
  147.5 0.1 div.30
  147.5 0.1 div.27
  147.6 0.0 copy-done.1
  147.6 0.6 add.24
  148.2 0.0 copy-done
  148.2 0.8 fusion
  (4 shorter events, 0.0 us)
Async XLA Ops:
  122.4 25.2 %copy-start.1 = (f32[1,512]{1,0:T(1,128)S(1)}, f32[1,512]{1,0:T(1,128)}, u32[]{:S(2)}) copy-start(f32[1,512]{1,0:T(1,128)} %param.7) | copy-start | bytes 6148
  122.4 25.8 %copy-start = (f32[1,512,128]{2,1,0:T(8,128)S(1)}, f32[1,512,128]{2,1,0:T(8,128)}, u32[]{:S(2)}) copy-start(f32[1,512,128]{2,1,0:T(8,128)} %param.6) | copy-start | bytes 786436

commit v2 on v1

v2 whole, which is shorter than its diff:
```python
import jax
import jax.numpy as jnp
from jax import lax
from jax.experimental import pallas as pl
from jax.experimental.pallas import tpu as pltpu
from jax.sharding import PartitionSpec as P

LEARN_RATE = 0.5
EPSILON = 1e-06


STEPS = 2


def accumulate_kernel(rows_ref, mult_ref, grads_ref, out_ref):
    step = pl.program_id(0)
    tiles = mult_ref.shape[0]

    @pl.when(step == 0)
    def _():
        out_ref[...] = jnp.zeros(out_ref.shape, out_ref.dtype)

    for t in range(tiles):
        contrib = lax.dot_general(
            mult_ref[t], grads_ref[t], (((0,), (0,)), ((), ())), preferred_element_type=jnp.float32
        )
        out_ref[rows_ref[step * tiles + t]] += contrib


def accumulate(row_ids, mult, grads, row_blocks):
    tiles, block, width = grads.shape
    tile_spec = pl.BlockSpec((tiles // STEPS, block, width), lambda i: (i, 0, 0))
    mult_spec = pl.BlockSpec((tiles // STEPS, block, block), lambda i: (i, 0, 0))
    return pl.pallas_call(
        accumulate_kernel,
        grid=(STEPS,),
        out_shape=jax.ShapeDtypeStruct((row_blocks, block, width), jnp.float32),
        in_specs=[pl.BlockSpec(memory_space=pltpu.SMEM), mult_spec, tile_spec],
        out_specs=pl.BlockSpec((row_blocks, block, width), lambda i: (0, 0, 0)),
        compiler_params=pltpu.CompilerParams(vmem_limit_bytes=16 << 20),
        name="accumulate",
    )(row_ids, mult, grads)


CORES = 2


def sum_over_replicas(partial_grad):
    rows, width = partial_grad.shape
    replicas = lax.axis_size("replica")
    chips = replicas // CORES
    core = lax.axis_index("replica") % CORES
    swap = [(i, i ^ 1) for i in range(replicas)]
    same_core = [[chip * CORES + c for chip in range(chips)] for c in range(CORES)]

    chip_sum = partial_grad + lax.ppermute(partial_grad, "replica", swap)
    half = lax.dynamic_index_in_dim(
        chip_sum.reshape(CORES, rows // CORES, width), core, 0, keepdims=False
    )
    copies = jnp.broadcast_to(half[None], (chips,) + half.shape)
    shares = lax.all_to_all(
        copies, "replica", split_axis=0, concat_axis=0, axis_index_groups=same_core, tiled=True
    )
    own = jnp.sum(shares, axis=0)
    other = lax.ppermute(own, "replica", swap)
    first = core == 0
    return jnp.concatenate([jnp.where(first, own, other), jnp.where(first, other, own)])


def adagrad(weights_in, accum_in, gradient):
    accum_out = accum_in + jnp.mean(gradient * gradient, axis=-1)
    weights_out = weights_in - LEARN_RATE * gradient / (jnp.sqrt(accum_out)[..., None] + EPSILON)
    return (weights_out, accum_out)


def on_device(pooled_grads, table, state, tile_mult, tile_rows):
    weights_in = table[0]
    accum_in = state[0]
    mult = tile_mult[0, 0]
    rows, width = weights_in.shape
    row_blocks = rows // mult.shape[-1]

    by_table = jnp.transpose(pooled_grads[0, 0], (1, 0, 2))
    received = lax.all_to_all(by_table, "mp", split_axis=0, concat_axis=0, tiled=True)
    partial_grad = accumulate(tile_rows[0, 0], mult, received, row_blocks)

    total_grad = sum_over_replicas(partial_grad.reshape(rows, width))

    weights_out, accum_out = adagrad(weights_in, accum_in, total_grad)
    return (weights_out[None], accum_out[None])


def solution(mesh):
    placed = (
        P("mp", "replica", None, None, None),
        P("mp", None, None),
        P("mp", None),
        P("mp", "replica", None, None, None),
        P("mp", "replica", None),
    )
    return jax.shard_map(
        on_device,
        mesh=mesh,
        in_specs=placed,
        out_specs=(P("mp", None, None), P("mp", None)),
        check_vma=False,
    )
```

time: 149 us -> 145 us (0.973)
  blocking collectives: 139 us -> 126 us
  starting transfers between devices: 0 us -> 9.54 us
  Pallas kernels: 5.15 us -> 1.58 us
  waiting for transfers between devices: 0 us -> 2.06 us
    all_to_all x2 -> x1, blocking collectives: 24.8 us -> 12.6 us  [sum_over_replicas(): lax.all_to_all(copies, 'replica', split_axis=0, concat_axis=0, axis_index...]
    ppermute x0 -> x2, starting transfers between devices: none -> 9.54 us  [the longest x1 5.83 us: sum_over_replicas(): chip_sum = partial_grad + lax.ppermute(partial_grad, 'replica', swap)]
    pallas_call x1, Pallas kernels: 5.15 us -> 1.58 us  [accumulate(): pl.pallas_call(accumulate_kernel, grid=(STEPS,), out_shape=jax.ShapeDtype...]
    ppermute x0 -> x2, waiting for transfers between devices: none -> 2.06 us  [the longest x1 1.1 us: sum_over_replicas(): chip_sum = partial_grad + lax.ppermute(partial_grad, 'replica', swap)]
  transfers between devices with their start and end apart: 0 -> 2, of which waited for: 0 -> 2; matrix products, arithmetic and copies ran while one was open for 0% -> 0% of each run, Pallas kernels for 0% -> 0%
where the time goes in v2:
time: 145 us
  blocking collectives  126 us (87%)
  starting transfers between devices  9.54 us (7%)
  local copies, waits for them, and re-layouts  3.02 us (2%)
  waiting for transfers between devices  2.06 us (1%)
  other arithmetic  1.66 us (1%)
  Pallas kernels  1.58 us (1%)
    all_to_all x1, blocking collectives, on_device(): lax.all_to_all(by_table, 'mp', split_axis=0, concat_axis=0, tiled=True)  114 us
    all_to_all x1, blocking collectives, sum_over_replicas(): lax.all_to_all(copies, 'replica', split_axis=0, concat_axis=0, axis_index...  12.6 us
    ppermute x1, starting transfers between devices, sum_over_replicas(): chip_sum = partial_grad + lax.ppermute(partial_grad, 'replica', swap)  5.83 us
    ppermute x1, starting transfers between devices, sum_over_replicas(): other = lax.ppermute(own, 'replica', swap)  3.71 us
    unnamed x9, local copies, waits for them, and re-layouts  2.97 us
  transfers between devices with their start and end apart: 2, of which 2 were waited for; matrix products, arithmetic and copies ran while one was open for 0% of the time, Pallas kernels for 0%

profile of v2, /device:TPU:1, one launch (start us, length us, event | category | flops | bytes accessed | tf_op | source)
XLA Modules:
  0.0 144.9 jit_solution(1053815369672864231)
XLA Ops:
  0.6 2.9 %copy.10 = bf16[1,1,128,64,128]{4,2,3,1,0:T(8,128)(2,1)S(1)} copy(bf16[1,1,128,64,128]{4,3,2,1,0:T(8,128)(2,1)} %param.5) | data formatting | bytes 4194304 | tf_op args[0]
  3.6 0.0 copy-start
  3.6 0.0 copy-start.1
  3.6 113.7 %all_to_all.10.grads_ref = bf16[64,128,128]{2,1,0:T(8,128)(2,1)S(1)} all-to-all(bf16[64,128,128]{2,1,0:T(8,128)(2,1)S(1)} %bitcast.19), channel_id=1, replica_groups=mesh['mp'=64,'replica'=8] {'mp'}, dimensions={0} | all-to-all | bytes 4194304 | tf_op jit(solution)/shard_map/all_to_all | solution.py:84
  117.3 0.0 copy-done
  117.3 0.0 copy-done.1
  117.3 1.6 %accumulate.1 = f32[4,128,128]{2,1,0:T(8,128)S(1)} custom-call(s32[64]{0:T(128)S(1)} %bitcast.18, bf16[64,128,128]{2,1,0:T(8,128)(2,1)S(1)} %bitcast.16, bf16[64,128,128]{2,1,0:T(8,128)(2,1)S(1)} %all_to_all.10.grads_ref), custom_call_target="tpu_custom_call" | custom-call | tf_op jit(solution)/shard_map/accumulate/pallas_call | solution.py:34
  118.9 5.8 %collective-permute-start = (f32[512,128]{1,0:T(8,128)S(1)}, f32[512,128]{1,0:T(8,128)S(1)}, u32[]{:S(2)}, u32[]{:S(2)}) collective-permute-start(f32[512,128]{1,0:T(8,128)S(1)} %bitcast.17), channel_id=1, source_target_pairs={{0,1},{1,0},{2,3},{3,2},{4,5},{5,4},{6,7},{7,6},{8,9},{9,8},{10,11... | collective-permute-start | bytes 786440 | tf_op jit(solution)/shard_map/ppermute | solution.py:56
  124.7 0.0 copy-start.3
  124.8 0.0 copy-start.2
  124.8 1.1 collective-permute-done
  126.0 12.6 %all_to_all.11 = f32[4,256,128]{2,1,0:T(8,128)S(1)} all-to-all(f32[4,256,128]{2,1,0:T(8,128)S(1)} %broadcast_in_dim.5), channel_id=1, replica_groups={{0,2,4,6},{1,3,5,7},{8,10,12,14},{9,11,13,15},{16,18,20,22},{17,19,21,2..., dimensions={0} | all-to-all | bytes 1048576 | tf_op jit(solution)/shard_map/all_to_all | solution.py:61
  138.6 3.7 %collective-permute-start.1 = (f32[256,128]{1,0:T(8,128)S(1)}, f32[256,128]{1,0:T(8,128)S(1)}, u32[]{:S(2)}, u32[]{:S(2)}) collective-permute-start(f32[256,128]{1,0:T(8,128)S(1)} %reduce_sum.18), channel_id=1, source_target_pairs={{0,1},{1,0},{2,3},{3,2},{4,5},{5,4},{6,7},{7,6},{8,9},{9,8},{10,11... | collective-permute-start | bytes 393224 | tf_op jit(solution)/shard_map/ppermute | solution.py:65
  142.3 1.0 collective-permute-done.1
  143.3 0.1 fusion.2
  143.5 0.0 copy-done.3
  143.5 0.6 add.38
  144.1 0.0 copy-done.2
  144.1 0.8 fusion.1
  (6 shorter events, 0.1 us)
Async XLA Ops:
  3.6 113.7 %copy-start = (bf16[1,1,64,128,128]{4,3,2,1,0:T(8,128)(2,1)S(1)}, bf16[1,1,64,128,128]{4,3,2,1,0:T(8,128)(2,1)}, u32[]{:S(2)}) copy-start(bf16[1,1,64,128,128]{4,3,2,1,0:T(8,128)(2,1)} %param.8) | copy-start | bytes 6291460
  3.6 113.7 %copy-start.1 = (s32[1,1,64]{2,1,0:T(1,128)S(1)}, s32[1,1,64]{2,1,0:T(1,128)}, u32[]{:S(2)}) copy-start(s32[1,1,64]{2,1,0:T(1,128)} %param.9) | copy-start | bytes 772
  118.9 7.0 %collective-permute-start = (f32[512,128]{1,0:T(8,128)S(1)}, f32[512,128]{1,0:T(8,128)S(1)}, u32[]{:S(2)}, u32[]{:S(2)}) collective-permute-start(f32[512,128]{1,0:T(8,128)S(1)} %bitcast.17), channel_id=1, source_target_pairs={{0,1},{1,0},{2,3},{3,2},{4,5},{5,4},{6,7},{7,6},{8,9},{9,8},{10,11... | collective-permute-start | bytes 786440 | tf_op jit(solution)/shard_map/ppermute | solution.py:56
  124.7 18.7 %copy-start.3 = (f32[1,512]{1,0:T(1,128)S(1)}, f32[1,512]{1,0:T(1,128)}, u32[]{:S(2)}) copy-start(f32[1,512]{1,0:T(1,128)} %param.7) | copy-start | bytes 6148
  124.8 19.3 %copy-start.2 = (f32[1,512,128]{2,1,0:T(8,128)S(1)}, f32[1,512,128]{2,1,0:T(8,128)}, u32[]{:S(2)}) copy-start(f32[1,512,128]{2,1,0:T(8,128)} %param.6) | copy-start | bytes 786436
  138.6 4.7 %collective-permute-start.1 = (f32[256,128]{1,0:T(8,128)S(1)}, f32[256,128]{1,0:T(8,128)S(1)}, u32[]{:S(2)}, u32[]{:S(2)}) collective-permute-start(f32[256,128]{1,0:T(8,128)S(1)} %reduce_sum.18), channel_id=1, source_target_pairs={{0,1},{1,0},{2,3},{3,2},{4,5},{5,4},{6,7},{7,6},{8,9},{9,8},{10,11... | collective-permute-start | bytes 393224 | tf_op jit(solution)/shard_map/ppermute | solution.py:65

commit v3 on v2

--- a/solution.py
+++ b/solution.py
@@ -7,42 +7,102 @@
 
 LEARN_RATE = 0.5
 EPSILON = 1e-06
-
-
-STEPS = 2
-
-
-def accumulate_kernel(rows_ref, mult_ref, grads_ref, out_ref):
-    step = pl.program_id(0)
-    tiles = mult_ref.shape[0]
-
-    @pl.when(step == 0)
-    def _():
-        out_ref[...] = jnp.zeros(out_ref.shape, out_ref.dtype)
-
-    for t in range(tiles):
-        contrib = lax.dot_general(
-            mult_ref[t], grads_ref[t], (((0,), (0,)), ((), ())), preferred_element_type=jnp.float32
-        )
-        out_ref[rows_ref[step * tiles + t]] += contrib
-
-
-def accumulate(row_ids, mult, grads, row_blocks):
-    tiles, block, width = grads.shape
-    tile_spec = pl.BlockSpec((tiles // STEPS, block, width), lambda i: (i, 0, 0))
-    mult_spec = pl.BlockSpec((tiles // STEPS, block, block), lambda i: (i, 0, 0))
+CORES = 2
+X = 4
+Z = 16
+HALF = Z // 2
+NEAR = (1, 2, 3)
+FAR = ((8, 7, 6), (5, 4))
+
+
+def vmem_specs(n):
+    return [pl.BlockSpec(memory_space=pltpu.VMEM)] * n
+
+
+SMEM = pl.BlockSpec(memory_space=pltpu.SMEM)
+PARAMS = pltpu.CompilerParams(vmem_limit_bytes=16 << 20)
+
+
+def relayout(src, row_ids, local):
+    samples, tables, width = local.shape
+    others = (HALF - 1) * X
+
+    def kernel(src_ref, rows_ref, in_ref, table_ref, half_ref, other_ref):
+        for g in range(X):
+            block = jnp.swapaxes(in_ref[:, g * Z : (g + 1) * Z, :], 0, 1)
+            table_ref[g * Z : (g + 1) * Z] = block
+        for j in range(X):
+            half_ref[j] = table_ref[src_ref[HALF * X + j]]
+        for n in range(others):
+            i, j = n // X + 1, n % X
+            other_ref[n] = table_ref[src_ref[(Z - i) * X + j]]
+        ids = rows_ref[...].astype(jnp.float32)
+        ids = jnp.concatenate([ids] * (width // ids.shape[1]), axis=1)
+        other_ref[others] = jnp.broadcast_to(ids, (samples, width)).astype(other_ref.dtype)
+
+    def out(n):
+        return jax.ShapeDtypeStruct((n, samples, width), local.dtype)
+
     return pl.pallas_call(
-        accumulate_kernel,
-        grid=(STEPS,),
+        kernel,
+        out_shape=[out(tables), out(X), out(others + 1)],
+        in_specs=[SMEM] + vmem_specs(2),
+        out_specs=vmem_specs(3),
+        compiler_params=PARAMS,
+        name="relayout",
+    )(src, row_ids[None], local)
+
+
+def regroup(src, inputs, plans):
+    block = inputs[0].shape[1:]
+
+    def kernel(src_ref, *refs):
+        in_refs, out_refs = refs[: len(inputs)], refs[len(inputs) :]
+        for out_ref, plan in zip(out_refs, plans):
+            for n, (i, k, *place) in enumerate(plan):
+                out_ref[n] = in_refs[i][src_ref[place[0]] if k is None else k]
+
+    return pl.pallas_call(
+        kernel,
+        out_shape=[jax.ShapeDtypeStruct((len(p),) + block, inputs[0].dtype) for p in plans],
+        in_specs=[SMEM] + vmem_specs(len(inputs)),
+        out_specs=vmem_specs(len(plans)),
+        compiler_params=PARAMS,
+        name="regroup",
+    )(src, *inputs)
+
+
+def add_tiles(partial, groups, tile, mult, rows, row_blocks):
+    blocks = [g for g, _ in groups]
+    pairs_of = [p for _, ps in groups for p in ps]
+    owner = [(n, k) for n, (_, ps) in enumerate(groups) for k in range(len(ps))]
+    block, width = blocks[0].shape[1:]
+
+    def kernel(tile_ref, rows0, rows1, mult0, mult1, *refs):
+        block_refs, out_ref = refs[: len(blocks)], refs[-1]
+        if partial is None:
+            out_ref[...] = jnp.zeros(out_ref.shape, out_ref.dtype)
+        else:
+            out_ref[...] = refs[-2][...]
+        for (i, j, s), (g, k) in zip(pairs_of, owner):
+            t = tile_ref[i * X + j]
+            mult_ref, rows_ref = (mult1, rows1) if s else (mult0, rows0)
+            out_ref[rows_ref[t]] += lax.dot_general(
+                mult_ref[t],
+                block_refs[g][k],
+                (((0,), (0,)), ((), ())),
+                preferred_element_type=jnp.float32,
+            )
+
+    start = [] if partial is None else [partial]
+    return pl.pallas_call(
+        kernel,
         out_shape=jax.ShapeDtypeStruct((row_blocks, block, width), jnp.float32),
-        in_specs=[pl.BlockSpec(memory_space=pltpu.SMEM), mult_spec, tile_spec],
-        out_specs=pl.BlockSpec((row_blocks, block, width), lambda i: (0, 0, 0)),
-        compiler_params=pltpu.CompilerParams(vmem_limit_bytes=16 << 20),
-        name="accumulate",
-    )(row_ids, mult, grads)
-
-
-CORES = 2
+        in_specs=[SMEM] * 3 + vmem_specs(2 + len(blocks) + len(start)),
+        out_specs=vmem_specs(1)[0],
+        compiler_params=PARAMS,
+        name="add_tiles",
+    )(tile, *rows, *mult, *blocks, *start)
 
 
 def sum_over_replicas(partial_grad):
@@ -73,19 +133,97 @@
     return (weights_out, accum_out)
 
 
+def pairs(shift):
+    replicas = 4 * CORES
+    out = []
+    for x in range(X):
+        for z in range(Z):
+            for r in range(replicas):
+                c = r % CORES
+                x2, z2, c2 = shift(x, z, c)
+                target = ((x2 % X) * Z + z2 % Z) * replicas + r - c + c2
+                out.append(((x * Z + z) * replicas + r, target))
+    return out
+
+
+def move(value, shift):
+    return lax.ppermute(value, ("mp", "replica"), pairs(shift))
+
+
+def over_z(i):
+    return lambda x, z, c: (x, z + (i if c == 0 else -i), c)
+
+
+def over_x(j):
+    return lambda x, z, c: (x + j, z, c)
+
+
+def other_core(x, z, c):
+    return (x, z, 1 - c)
+
+
+def exchange_and_add(local, mult, rows, row_blocks):
+    mp = lax.axis_index("mp")
+    x, z = mp // Z, mp % Z
+    core = lax.axis_index("replica") % CORES
+    way = 1 - 2 * core
+    place = jnp.arange(Z * X, dtype=jnp.int32)
+    shift, step = place // X, place % X
+    src = (x + step) % X * Z + (z + way * shift) % Z
+    tile = (x - step) % X * Z + (z - way * shift) % Z
+
+    by_table, half, oth = relayout(src, rows, local)
+    got = {HALF: move(half, over_z(HALF))}
+    sib = move(oth, other_core)
+    rows = (rows, sib[-1, 0, : rows.shape[0]].astype(jnp.int32))
+
+    def both(i, j):
+        return [(0, None, i * X + j), (1, (i - 1) * X + j)]
+
+    far_shifts = (7, 6, 5, 4)
+    plans = [[both(i, j)[s] for s in range(2) for j in range(X)] for i in far_shifts]
+    plans += [[(0, None, j)] + [b for i in NEAR for b in both(i, j)] for j in range(X)]
+    made = regroup(src, [by_table, sib], plans)
+    mine, near = dict(zip(far_shifts, made)), list(made[len(far_shifts) :])
+    for i in (7, 6):
+        got[i] = move(mine[i], over_z(i))
+    for j in range(1, X):
+        near[j] = move(near[j], over_x(j))
+    for i in (5, 4):
+        got[i] = move(mine[i], over_z(i))
+    mult = (mult, move(mult, other_core))
+
+    def far(shifts):
+        who = [(n, i, s) for n, i in enumerate(shifts) for s in range(1 if i == HALF else 2)]
+        plans = [[(n, s * X + j) for n, _, s in who] for j in range(X)]
+        made = list(regroup(src, [got[i] for i in shifts], plans))
+        for j in range(1, X):
+            made[j] = move(made[j], over_x(j))
+        return [(made[j], [(i, j, s) for _, i, s in who]) for j in range(X)]
+
+    groups = [(near[j], [(0, j, 0)]) for j in range(X)]
+    groups += far(FAR[0])
+    plans = [
+        [(j, 1 + 2 * NEAR.index(i) + s) for s in range(2) for j in range(X)] for i in NEAR
+    ]
+    made = regroup(src, near, plans)
+    last = []
+    for i in NEAR[::-1]:
+        blocks = move(made[NEAR.index(i)], over_z(i))
+        last.append((blocks, [(i, j, s) for s in range(2) for j in range(X)]))
+    groups += far(FAR[1])
+    partial = add_tiles(None, groups, tile, mult, rows, row_blocks)
+    return add_tiles(partial, last, tile, mult, rows, row_blocks)
+
+
 def on_device(pooled_grads, table, state, tile_mult, tile_rows):
     weights_in = table[0]
     accum_in = state[0]
     mult = tile_mult[0, 0]
     rows, width = weights_in.shape
     row_blocks = rows // mult.shape[-1]
-
-    by_table = jnp.transpose(pooled_grads[0, 0], (1, 0, 2))
-    received = lax.all_to_all(by_table, "mp", split_axis=0, concat_axis=0, tiled=True)
-    partial_grad = accumulate(tile_rows[0, 0], mult, received, row_blocks)
-
+    partial_grad = exchange_and_add(pooled_grads[0, 0], mult, tile_rows[0, 0], row_blocks)
     total_grad = sum_over_replicas(partial_grad.reshape(rows, width))
-
     weights_out, accum_out = adagrad(weights_in, accum_in, total_grad)
     return (weights_out[None], accum_out[None])
 

time: 145 us -> 176 us (1.21)
  blocking collectives: 126 us -> 12.6 us
  starting transfers between devices: 9.54 us -> 120 us
  waiting for transfers between devices: 2.06 us -> 31.4 us
  Pallas kernels: 1.58 us -> 6.19 us
    all_to_all x1 -> x0, blocking collectives: 114 us -> none  [on_device(): lax.all_to_all(by_table, 'mp', split_axis=0, concat_axis=0, tiled=True)]
    ppermute x0 -> x19, starting transfers between devices: none -> 112 us  [move(): return lax.ppermute(value, ('mp', 'replica'), pairs(shift))]
    ppermute x0 -> x19, waiting for transfers between devices: none -> 29.3 us  [move(): return lax.ppermute(value, ('mp', 'replica'), pairs(shift))]
    pallas_call x1 -> x7, Pallas kernels: 1.58 us -> 6.19 us  [the longest x4 2.42 us: regroup(): pl.pallas_call(kernel, out_shape=[jax.ShapeDtypeStruct((len(p),) + block,...]
  transfers between devices with their start and end apart: 2 -> 21, of which waited for: 2 -> 7; matrix products, arithmetic and copies ran while one was open for 0% -> 0% of each run, Pallas kernels for 0% -> 3%
where the time goes in v3:
time: 176 us; the launch traced here: 175 us
  starting transfers between devices  120 us (68%)
  waiting for transfers between devices  31.4 us (18%)
  blocking collectives  12.6 us (7%)
  Pallas kernels  6.19 us (4%)
  local copies, waits for them, and re-layouts  2.31 us (1%)
    ppermute x19, starting transfers between devices, move(): return lax.ppermute(value, ('mp', 'replica'), pairs(shift))  112 us
    ppermute x19, waiting for transfers between devices, move(): return lax.ppermute(value, ('mp', 'replica'), pairs(shift))  29.3 us
    all_to_all x1, blocking collectives, sum_over_replicas(): lax.all_to_all(copies, 'replica', split_axis=0, concat_axis=0, axis_index...  12.6 us
    ppermute x1, starting transfers between devices, sum_over_replicas(): chip_sum = partial_grad + lax.ppermute(partial_grad, 'replica', swap)  4.21 us
    ppermute x1, starting transfers between devices, sum_over_replicas(): other = lax.ppermute(own, 'replica', swap)  3.71 us
  transfers between devices with their start and end apart: 21, of which 7 were waited for; matrix products, arithmetic and copies ran while one was open for 0% of the time, Pallas kernels for 3%

profile of v3, /device:TPU:1, one launch (start us, length us, event | category | flops | bytes accessed | tf_op | source)
XLA Modules:
  0.0 175.0 jit_solution(14472455906095929956)
XLA Ops:
  0.6 8.7 %collective-permute-start.1 = (bf16[64,128,128]{2,1,0:T(8,128)(2,1)}, bf16[64,128,128]{2,1,0:T(8,128)(2,1)S(1)}, u32[]{:S(2)}, u32[]{:S(2)}) collective-permute-start(bf16[64,128,128]{2,1,0:T(8,128)(2,1)} %bitcast.18), channel_id=1, source_target_pairs={{0,1},{1,0},{2,3},{3,2},{4,5},{5,4},{6,7},{7,6},{8,9},{9,8},{10,11... | collective-permute-start | bytes 6291464 | tf_op jit(solution)/shard_map/ppermute | solution.py:150
  9.4 0.0 copy-start.1
  9.4 1.6 copy-done.1
  11.0 0.7 copy-done.2
  11.7 1.6 relayout.1
  13.3 1.9 %collective-permute-start = (bf16[29,128,128]{2,1,0:T(8,128)(2,1)S(1)}, bf16[29,128,128]{2,1,0:T(8,128)(2,1)S(1)}, u32[]{:S(2)}, u32[]{:S(2)}) collective-permute-start(bf16[29,128,128]{2,1,0:T(8,128)(2,1)S(1)} %get-tuple-element.24), channel_id=1, source_target_pairs={{0,1},{1,0},{2,3},{3,2},{4,5},{5,4},{6,7},{7,6},{8,9},{9,8},{10,11... | collective-permute-start | bytes 2850824 | tf_op jit(solution)/shard_map/ppermute | solution.py:150
  15.2 2.5 %collective-permute-done.refs_1_ = bf16[29,128,128]{2,1,0:T(8,128)(2,1)S(1)} collective-permute-done((bf16[29,128,128]{2,1,0:T(8,128)(2,1)S(1)}, bf16[29,128,128]{2,1,0:T(8,128)(2,1)S(1)}, u32[]{:S(2)}, u32[]{:S(2)}) %collective-permute-start) | collective-permute-done | bytes 950304 | tf_op jit(solution)/shard_map/ppermute | solution.py:150
  17.7 0.7 regroup.4
  18.4 8.8 %collective-permute-start.14 = (bf16[8,128,128]{2,1,0:T(8,128)(2,1)S(1)}, bf16[8,128,128]{2,1,0:T(8,128)(2,1)S(1)}, u32[]{:S(2)}, u32[]{:S(2)}) collective-permute-start(bf16[8,128,128]{2,1,0:T(8,128)(2,1)S(1)} %get-tuple-element.40), channel_id=1, source_target_pairs={{0,40},{1,89},{2,42},{3,91},{4,44},{5,93},{6,46},{7,95},{8,48},{9,... | collective-permute-start | bytes 786440 | tf_op jit(solution)/shard_map/ppermute | solution.py:150
  27.2 3.1 %collective-permute-start.15 = (bf16[8,128,128]{2,1,0:T(8,128)(2,1)S(1)}, bf16[8,128,128]{2,1,0:T(8,128)(2,1)S(1)}, u32[]{:S(2)}, u32[]{:S(2)}) collective-permute-start(bf16[8,128,128]{2,1,0:T(8,128)(2,1)S(1)} %get-tuple-element.41), channel_id=1, source_target_pairs={{0,32},{1,97},{2,34},{3,99},{4,36},{5,101},{6,38},{7,103},{8,40},{... | collective-permute-start | bytes 786440 | tf_op jit(solution)/shard_map/ppermute | solution.py:150
  30.3 1.9 %collective-permute-start.10 = (bf16[8,128,128]{2,1,0:T(8,128)(2,1)S(1)}, bf16[8,128,128]{2,1,0:T(8,128)(2,1)S(1)}, u32[]{:S(2)}, u32[]{:S(2)}) collective-permute-start(bf16[8,128,128]{2,1,0:T(8,128)(2,1)S(1)} %get-tuple-element.35), channel_id=1, source_target_pairs={{0,48},{1,81},{2,50},{3,83},{4,52},{5,85},{6,54},{7,87},{8,56},{9,... | collective-permute-start | bytes 786440 | tf_op jit(solution)/shard_map/ppermute | solution.py:150
  32.2 12.1 %collective-permute-start.8 = (bf16[4,128,128]{2,1,0:T(8,128)(2,1)S(1)}, bf16[4,128,128]{2,1,0:T(8,128)(2,1)S(1)}, u32[]{:S(2)}, u32[]{:S(2)}) collective-permute-start(bf16[4,128,128]{2,1,0:T(8,128)(2,1)S(1)} %get-tuple-element.33), channel_id=1, source_target_pairs={{0,64},{1,65},{2,66},{3,67},{4,68},{5,69},{6,70},{7,71},{8,72},{9,... | collective-permute-start | bytes 393224 | tf_op jit(solution)/shard_map/ppermute | solution.py:150
  44.3 20.5 %collective-permute-done.8.refs_0_ = bf16[4,128,128]{2,1,0:T(8,128)(2,1)S(1)} collective-permute-done((bf16[4,128,128]{2,1,0:T(8,128)(2,1)S(1)}, bf16[4,128,128]{2,1,0:T(8,128)(2,1)S(1)}, u32[]{:S(2)}, u32[]{:S(2)}) %collective-permute-start.8) | collective-permute-done | bytes 131104 | tf_op jit(solution)/shard_map/ppermute | solution.py:150
  64.8 27.3 %collective-permute-start.9 = (bf16[8,128,128]{2,1,0:T(8,128)(2,1)S(1)}, bf16[8,128,128]{2,1,0:T(8,128)(2,1)S(1)}, u32[]{:S(2)}, u32[]{:S(2)}) collective-permute-start(bf16[8,128,128]{2,1,0:T(8,128)(2,1)S(1)} %get-tuple-element.34), channel_id=1, source_target_pairs={{0,56},{1,73},{2,58},{3,75},{4,60},{5,77},{6,62},{7,79},{8,64},{9,... | collective-permute-start | bytes 786440 | tf_op jit(solution)/shard_map/ppermute | solution.py:150
  92.0 0.0 collective-permute-done.14.refs_0_
  92.1 1.9 %collective-permute-start.2 = (bf16[7,128,128]{2,1,0:T(8,128)(2,1)S(1)}, bf16[7,128,128]{2,1,0:T(8,128)(2,1)S(1)}, u32[]{:S(2)}, u32[]{:S(2)}) collective-permute-start(bf16[7,128,128]{2,1,0:T(8,128)(2,1)S(1)} %get-tuple-element.27), channel_id=1, source_target_pairs={{0,128},{1,129},{2,130},{3,131},{4,132},{5,133},{6,134},{7,135},{8... | collective-permute-start | bytes 688136 | tf_op jit(solution)/shard_map/ppermute | solution.py:150
  94.0 19.3 %collective-permute-start.3 = (bf16[7,128,128]{2,1,0:T(8,128)(2,1)S(1)}, bf16[7,128,128]{2,1,0:T(8,128)(2,1)S(1)}, u32[]{:S(2)}, u32[]{:S(2)}) collective-permute-start(bf16[7,128,128]{2,1,0:T(8,128)(2,1)S(1)} %get-tuple-element.28), channel_id=1, source_target_pairs={{0,256},{1,257},{2,258},{3,259},{4,260},{5,261},{6,262},{7,263},{8... | collective-permute-start | bytes 688136 | tf_op jit(solution)/shard_map/ppermute | solution.py:150
  113.3 0.0 collective-permute-done.10.refs_2_
  113.3 1.9 %collective-permute-start.4 = (bf16[7,128,128]{2,1,0:T(8,128)(2,1)S(1)}, bf16[7,128,128]{2,1,0:T(8,128)(2,1)S(1)}, u32[]{:S(2)}, u32[]{:S(2)}) collective-permute-start(bf16[7,128,128]{2,1,0:T(8,128)(2,1)S(1)} %get-tuple-element.29), channel_id=1, source_target_pairs={{0,384},{1,385},{2,386},{3,387},{4,388},{5,389},{6,390},{7,391},{8... | collective-permute-start | bytes 688136 | tf_op jit(solution)/shard_map/ppermute | solution.py:150
  115.2 0.6 regroup.7
  115.8 3.4 %collective-permute-start.16 = (bf16[4,128,128]{2,1,0:T(8,128)(2,1)S(1)}, bf16[4,128,128]{2,1,0:T(8,128)(2,1)S(1)}, u32[]{:S(2)}, u32[]{:S(2)}) collective-permute-start(bf16[4,128,128]{2,1,0:T(8,128)(2,1)S(1)} %get-tuple-element.43), channel_id=1, source_target_pairs={{0,128},{1,129},{2,130},{3,131},{4,132},{5,133},{6,134},{7,135},{8... | collective-permute-start | bytes 393224 | tf_op jit(solution)/shard_map/ppermute | solution.py:150
  119.2 0.6 regroup.6
  119.8 1.9 %collective-permute-start.11 = (bf16[5,128,128]{2,1,0:T(8,128)(2,1)S(1)}, bf16[5,128,128]{2,1,0:T(8,128)(2,1)S(1)}, u32[]{:S(2)}, u32[]{:S(2)}) collective-permute-start(bf16[5,128,128]{2,1,0:T(8,128)(2,1)S(1)} %get-tuple-element.37), channel_id=1, source_target_pairs={{0,128},{1,129},{2,130},{3,131},{4,132},{5,133},{6,134},{7,135},{8... | collective-permute-start | bytes 491528 | tf_op jit(solution)/shard_map/ppermute | solution.py:150
  121.7 0.0 collective-permute-done.3.refs_2_
  121.7 4.3 %collective-permute-start.17 = (bf16[4,128,128]{2,1,0:T(8,128)(2,1)S(1)}, bf16[4,128,128]{2,1,0:T(8,128)(2,1)S(1)}, u32[]{:S(2)}, u32[]{:S(2)}) collective-permute-start(bf16[4,128,128]{2,1,0:T(8,128)(2,1)S(1)} %get-tuple-element.44), channel_id=1, source_target_pairs={{0,256},{1,257},{2,258},{3,259},{4,260},{5,261},{6,262},{7,263},{8... | collective-permute-start | bytes 393224 | tf_op jit(solution)/shard_map/ppermute | solution.py:150
  126.0 0.0 collective-permute-done.4.refs_3_
  126.0 2.2 %collective-permute-start.18 = (bf16[4,128,128]{2,1,0:T(8,128)(2,1)S(1)}, bf16[4,128,128]{2,1,0:T(8,128)(2,1)S(1)}, u32[]{:S(2)}, u32[]{:S(2)}) collective-permute-start(bf16[4,128,128]{2,1,0:T(8,128)(2,1)S(1)} %get-tuple-element.45), channel_id=1, source_target_pairs={{0,384},{1,385},{2,386},{3,387},{4,388},{5,389},{6,390},{7,391},{8... | collective-permute-start | bytes 393224 | tf_op jit(solution)/shard_map/ppermute | solution.py:150
  128.2 4.3 %collective-permute-start.12 = (bf16[5,128,128]{2,1,0:T(8,128)(2,1)S(1)}, bf16[5,128,128]{2,1,0:T(8,128)(2,1)S(1)}, u32[]{:S(2)}, u32[]{:S(2)}) collective-permute-start(bf16[5,128,128]{2,1,0:T(8,128)(2,1)S(1)} %get-tuple-element.38), channel_id=1, source_target_pairs={{0,256},{1,257},{2,258},{3,259},{4,260},{5,261},{6,262},{7,263},{8... | collective-permute-start | bytes 491528 | tf_op jit(solution)/shard_map/ppermute | solution.py:150
  132.5 0.6 regroup.5
  133.1 1.9 %collective-permute-start.5 = (bf16[8,128,128]{2,1,0:T(8,128)(2,1)S(1)}, bf16[8,128,128]{2,1,0:T(8,128)(2,1)S(1)}, u32[]{:S(2)}, u32[]{:S(2)}) collective-permute-start(bf16[8,128,128]{2,1,0:T(8,128)(2,1)S(1)} %get-tuple-element.30), channel_id=1, source_target_pairs={{0,24},{1,105},{2,26},{3,107},{4,28},{5,109},{6,30},{7,111},{8,32}... | collective-permute-start | bytes 786440 | tf_op jit(solution)/shard_map/ppermute | solution.py:150
  135.1 1.9 %collective-permute-start.6 = (bf16[8,128,128]{2,1,0:T(8,128)(2,1)S(1)}, bf16[8,128,128]{2,1,0:T(8,128)(2,1)S(1)}, u32[]{:S(2)}, u32[]{:S(2)}) collective-permute-start(bf16[8,128,128]{2,1,0:T(8,128)(2,1)S(1)} %get-tuple-element.31), channel_id=1, source_target_pairs={{0,16},{1,113},{2,18},{3,115},{4,20},{5,117},{6,22},{7,119},{8,24}... | collective-permute-start | bytes 786440 | tf_op jit(solution)/shard_map/ppermute | solution.py:150
  137.0 1.9 %collective-permute-start.7 = (bf16[8,128,128]{2,1,0:T(8,128)(2,1)S(1)}, bf16[8,128,128]{2,1,0:T(8,128)(2,1)S(1)}, u32[]{:S(2)}, u32[]{:S(2)}) collective-permute-start(bf16[8,128,128]{2,1,0:T(8,128)(2,1)S(1)} %get-tuple-element.32), channel_id=1, source_target_pairs={{0,8},{1,121},{2,10},{3,123},{4,12},{5,125},{6,14},{7,127},{8,16},... | collective-permute-start | bytes 786440 | tf_op jit(solution)/shard_map/ppermute | solution.py:150
  139.0 3.1 %collective-permute-start.13 = (bf16[5,128,128]{2,1,0:T(8,128)(2,1)S(1)}, bf16[5,128,128]{2,1,0:T(8,128)(2,1)S(1)}, u32[]{:S(2)}, u32[]{:S(2)}) collective-permute-start(bf16[5,128,128]{2,1,0:T(8,128)(2,1)S(1)} %get-tuple-element.39), channel_id=1, source_target_pairs={{0,384},{1,385},{2,386},{3,387},{4,388},{5,389},{6,390},{7,391},{8... | collective-permute-start | bytes 491528 | tf_op jit(solution)/shard_map/ppermute | solution.py:150
  142.1 3.2 %collective-permute-done.13.refs_7_ = bf16[5,128,128]{2,1,0:T(8,128)(2,1)S(1)} collective-permute-done((bf16[5,128,128]{2,1,0:T(8,128)(2,1)S(1)}, bf16[5,128,128]{2,1,0:T(8,128)(2,1)S(1)}, u32[]{:S(2)}, u32[]{:S(2)}) %collective-permute-start.13) | collective-permute-done | bytes 163872 | tf_op jit(solution)/shard_map/ppermute | solution.py:150
  145.3 1.2 add_tiles.2.refs_3_
  146.5 0.9 collective-permute-done.5.refs_0_
  147.4 2.2 %collective-permute-done.7.refs_2_ = bf16[8,128,128]{2,1,0:T(8,128)(2,1)S(1)} collective-permute-done((bf16[8,128,128]{2,1,0:T(8,128)(2,1)S(1)}, bf16[8,128,128]{2,1,0:T(8,128)(2,1)S(1)}, u32[]{:S(2)}, u32[]{:S(2)}) %collective-permute-start.7) | collective-permute-done | bytes 262176 | tf_op jit(solution)/shard_map/ppermute | solution.py:150
  149.6 1.0 add_tiles.3
  150.6 4.2 %collective-permute-start.19 = (f32[512,128]{1,0:T(8,128)S(1)}, f32[512,128]{1,0:T(8,128)S(1)}, u32[]{:S(2)}, u32[]{:S(2)}) collective-permute-start(f32[512,128]{1,0:T(8,128)S(1)} %bitcast.22), channel_id=1, source_target_pairs={{0,1},{1,0},{2,3},{3,2},{4,5},{5,4},{6,7},{7,6},{8,9},{9,8},{10,11... | collective-permute-start | bytes 786440 | tf_op jit(solution)/shard_map/ppermute | solution.py:116
  154.8 0.0 copy-start.4
  154.8 0.0 copy-start.3
  154.9 1.1 collective-permute-done.19
  156.1 12.6 %all_to_all.5 = f32[4,256,128]{2,1,0:T(8,128)S(1)} all-to-all(f32[4,256,128]{2,1,0:T(8,128)S(1)} %broadcast_in_dim.5), channel_id=1, replica_groups={{0,2,4,6},{1,3,5,7},{8,10,12,14},{9,11,13,15},{16,18,20,22},{17,19,21,2..., dimensions={0} | all-to-all | bytes 1048576 | tf_op jit(solution)/shard_map/all_to_all | solution.py:121
  168.7 3.7 %collective-permute-start.20 = (f32[256,128]{1,0:T(8,128)S(1)}, f32[256,128]{1,0:T(8,128)S(1)}, u32[]{:S(2)}, u32[]{:S(2)}) collective-permute-start(f32[256,128]{1,0:T(8,128)S(1)} %reduce_sum.18), channel_id=1, source_target_pairs={{0,1},{1,0},{2,3},{3,2},{4,5},{5,4},{6,7},{7,6},{8,9},{9,8},{10,11... | collective-permute-start | bytes 393224 | tf_op jit(solution)/shard_map/ppermute | solution.py:125
  172.4 1.0 collective-permute-done.20
  173.4 0.1 fusion.2
  173.6 0.6 add.92
  174.2 0.8 fusion.1
  (24 shorter events, 0.2 us)
Async XLA Ops:
  0.6 144.7 %collective-permute-start.1 = (bf16[64,128,128]{2,1,0:T(8,128)(2,1)}, bf16[64,128,128]{2,1,0:T(8,128)(2,1)S(1)}, u32[]{:S(2)}, u32[]{:S(2)}) collective-permute-start(bf16[64,128,128]{2,1,0:T(8,128)(2,1)} %bitcast.18), channel_id=1, source_target_pairs={{0,1},{1,0},{2,3},{3,2},{4,5},{5,4},{6,7},{7,6},{8,9},{9,8},{10,11... | collective-permute-start | bytes 6291464 | tf_op jit(solution)/shard_map/ppermute | solution.py:150
  9.4 1.6 copy-start.1
  11.0 0.7 copy-start.2
  13.3 4.4 %collective-permute-start = (bf16[29,128,128]{2,1,0:T(8,128)(2,1)S(1)}, bf16[29,128,128]{2,1,0:T(8,128)(2,1)S(1)}, u32[]{:S(2)}, u32[]{:S(2)}) collective-permute-start(bf16[29,128,128]{2,1,0:T(8,128)(2,1)S(1)} %get-tuple-element.24), channel_id=1, source_target_pairs={{0,1},{1,0},{2,3},{3,2},{4,5},{5,4},{6,7},{7,6},{8,9},{9,8},{10,11... | collective-permute-start | bytes 2850824 | tf_op jit(solution)/shard_map/ppermute | solution.py:150
  17.7 127.6 %copy-start = (bf16[1,1,64,128,128]{4,3,2,1,0:T(8,128)(2,1)S(1)}, bf16[1,1,64,128,128]{4,3,2,1,0:T(8,128)(2,1)}, u32[]{:S(2)}) copy-start(bf16[1,1,64,128,128]{4,3,2,1,0:T(8,128)(2,1)} %param.8) | copy-start | bytes 6291460
  18.4 73.6 %collective-permute-start.14 = (bf16[8,128,128]{2,1,0:T(8,128)(2,1)S(1)}, bf16[8,128,128]{2,1,0:T(8,128)(2,1)S(1)}, u32[]{:S(2)}, u32[]{:S(2)}) collective-permute-start(bf16[8,128,128]{2,1,0:T(8,128)(2,1)S(1)} %get-tuple-element.40), channel_id=1, source_target_pairs={{0,40},{1,89},{2,42},{3,91},{4,44},{5,93},{6,46},{7,95},{8,48},{9,... | collective-permute-start | bytes 786440 | tf_op jit(solution)/shard_map/ppermute | solution.py:150
  27.2 66.8 %collective-permute-start.15 = (bf16[8,128,128]{2,1,0:T(8,128)(2,1)S(1)}, bf16[8,128,128]{2,1,0:T(8,128)(2,1)S(1)}, u32[]{:S(2)}, u32[]{:S(2)}) collective-permute-start(bf16[8,128,128]{2,1,0:T(8,128)(2,1)S(1)} %get-tuple-element.41), channel_id=1, source_target_pairs={{0,32},{1,97},{2,34},{3,99},{4,36},{5,101},{6,38},{7,103},{8,40},{... | collective-permute-start | bytes 786440 | tf_op jit(solution)/shard_map/ppermute | solution.py:150
  30.3 83.0 %collective-permute-start.10 = (bf16[8,128,128]{2,1,0:T(8,128)(2,1)S(1)}, bf16[8,128,128]{2,1,0:T(8,128)(2,1)S(1)}, u32[]{:S(2)}, u32[]{:S(2)}) collective-permute-start(bf16[8,128,128]{2,1,0:T(8,128)(2,1)S(1)} %get-tuple-element.35), channel_id=1, source_target_pairs={{0,48},{1,81},{2,50},{3,83},{4,52},{5,85},{6,54},{7,87},{8,56},{9,... | collective-permute-start | bytes 786440 | tf_op jit(solution)/shard_map/ppermute | solution.py:150
  32.2 32.6 %collective-permute-start.8 = (bf16[4,128,128]{2,1,0:T(8,128)(2,1)S(1)}, bf16[4,128,128]{2,1,0:T(8,128)(2,1)S(1)}, u32[]{:S(2)}, u32[]{:S(2)}) collective-permute-start(bf16[4,128,128]{2,1,0:T(8,128)(2,1)S(1)} %get-tuple-element.33), channel_id=1, source_target_pairs={{0,64},{1,65},{2,66},{3,67},{4,68},{5,69},{6,70},{7,71},{8,72},{9,... | collective-permute-start | bytes 393224 | tf_op jit(solution)/shard_map/ppermute | solution.py:150
  64.8 51.0 %collective-permute-start.9 = (bf16[8,128,128]{2,1,0:T(8,128)(2,1)S(1)}, bf16[8,128,128]{2,1,0:T(8,128)(2,1)S(1)}, u32[]{:S(2)}, u32[]{:S(2)}) collective-permute-start(bf16[8,128,128]{2,1,0:T(8,128)(2,1)S(1)} %get-tuple-element.34), channel_id=1, source_target_pairs={{0,56},{1,73},{2,58},{3,75},{4,60},{5,77},{6,62},{7,79},{8,64},{9,... | collective-permute-start | bytes 786440 | tf_op jit(solution)/shard_map/ppermute | solution.py:150
  92.1 27.7 %collective-permute-start.2 = (bf16[7,128,128]{2,1,0:T(8,128)(2,1)S(1)}, bf16[7,128,128]{2,1,0:T(8,128)(2,1)S(1)}, u32[]{:S(2)}, u32[]{:S(2)}) collective-permute-start(bf16[7,128,128]{2,1,0:T(8,128)(2,1)S(1)} %get-tuple-element.27), channel_id=1, source_target_pairs={{0,128},{1,129},{2,130},{3,131},{4,132},{5,133},{6,134},{7,135},{8... | collective-permute-start | bytes 688136 | tf_op jit(solution)/shard_map/ppermute | solution.py:150
  94.0 27.7 %collective-permute-start.3 = (bf16[7,128,128]{2,1,0:T(8,128)(2,1)S(1)}, bf16[7,128,128]{2,1,0:T(8,128)(2,1)S(1)}, u32[]{:S(2)}, u32[]{:S(2)}) collective-permute-start(bf16[7,128,128]{2,1,0:T(8,128)(2,1)S(1)} %get-tuple-element.28), channel_id=1, source_target_pairs={{0,256},{1,257},{2,258},{3,259},{4,260},{5,261},{6,262},{7,263},{8... | collective-permute-start | bytes 688136 | tf_op jit(solution)/shard_map/ppermute | solution.py:150
  113.3 12.7 %collective-permute-start.4 = (bf16[7,128,128]{2,1,0:T(8,128)(2,1)S(1)}, bf16[7,128,128]{2,1,0:T(8,128)(2,1)S(1)}, u32[]{:S(2)}, u32[]{:S(2)}) collective-permute-start(bf16[7,128,128]{2,1,0:T(8,128)(2,1)S(1)} %get-tuple-element.29), channel_id=1, source_target_pairs={{0,384},{1,385},{2,386},{3,387},{4,388},{5,389},{6,390},{7,391},{8... | collective-permute-start | bytes 688136 | tf_op jit(solution)/shard_map/ppermute | solution.py:150
  115.8 12.4 %collective-permute-start.16 = (bf16[4,128,128]{2,1,0:T(8,128)(2,1)S(1)}, bf16[4,128,128]{2,1,0:T(8,128)(2,1)S(1)}, u32[]{:S(2)}, u32[]{:S(2)}) collective-permute-start(bf16[4,128,128]{2,1,0:T(8,128)(2,1)S(1)} %get-tuple-element.43), channel_id=1, source_target_pairs={{0,128},{1,129},{2,130},{3,131},{4,132},{5,133},{6,134},{7,135},{8... | collective-permute-start | bytes 393224 | tf_op jit(solution)/shard_map/ppermute | solution.py:150
  119.8 17.2 %collective-permute-start.11 = (bf16[5,128,128]{2,1,0:T(8,128)(2,1)S(1)}, bf16[5,128,128]{2,1,0:T(8,128)(2,1)S(1)}, u32[]{:S(2)}, u32[]{:S(2)}) collective-permute-start(bf16[5,128,128]{2,1,0:T(8,128)(2,1)S(1)} %get-tuple-element.37), channel_id=1, source_target_pairs={{0,128},{1,129},{2,130},{3,131},{4,132},{5,133},{6,134},{7,135},{8... | collective-permute-start | bytes 491528 | tf_op jit(solution)/shard_map/ppermute | solution.py:150
  121.7 11.4 %collective-permute-start.17 = (bf16[4,128,128]{2,1,0:T(8,128)(2,1)S(1)}, bf16[4,128,128]{2,1,0:T(8,128)(2,1)S(1)}, u32[]{:S(2)}, u32[]{:S(2)}) collective-permute-start(bf16[4,128,128]{2,1,0:T(8,128)(2,1)S(1)} %get-tuple-element.44), channel_id=1, source_target_pairs={{0,256},{1,257},{2,258},{3,259},{4,260},{5,261},{6,262},{7,263},{8... | collective-permute-start | bytes 393224 | tf_op jit(solution)/shard_map/ppermute | solution.py:150
  126.0 9.0 %collective-permute-start.18 = (bf16[4,128,128]{2,1,0:T(8,128)(2,1)S(1)}, bf16[4,128,128]{2,1,0:T(8,128)(2,1)S(1)}, u32[]{:S(2)}, u32[]{:S(2)}) collective-permute-start(bf16[4,128,128]{2,1,0:T(8,128)(2,1)S(1)} %get-tuple-element.45), channel_id=1, source_target_pairs={{0,384},{1,385},{2,386},{3,387},{4,388},{5,389},{6,390},{7,391},{8... | collective-permute-start | bytes 393224 | tf_op jit(solution)/shard_map/ppermute | solution.py:150
  128.2 10.7 %collective-permute-start.12 = (bf16[5,128,128]{2,1,0:T(8,128)(2,1)S(1)}, bf16[5,128,128]{2,1,0:T(8,128)(2,1)S(1)}, u32[]{:S(2)}, u32[]{:S(2)}) collective-permute-start(bf16[5,128,128]{2,1,0:T(8,128)(2,1)S(1)} %get-tuple-element.38), channel_id=1, source_target_pairs={{0,256},{1,257},{2,258},{3,259},{4,260},{5,261},{6,262},{7,263},{8... | collective-permute-start | bytes 491528 | tf_op jit(solution)/shard_map/ppermute | solution.py:150
  133.1 14.3 %collective-permute-start.5 = (bf16[8,128,128]{2,1,0:T(8,128)(2,1)S(1)}, bf16[8,128,128]{2,1,0:T(8,128)(2,1)S(1)}, u32[]{:S(2)}, u32[]{:S(2)}) collective-permute-start(bf16[8,128,128]{2,1,0:T(8,128)(2,1)S(1)} %get-tuple-element.30), channel_id=1, source_target_pairs={{0,24},{1,105},{2,26},{3,107},{4,28},{5,109},{6,30},{7,111},{8,32}... | collective-permute-start | bytes 786440 | tf_op jit(solution)/shard_map/ppermute | solution.py:150
  135.1 12.4 %collective-permute-start.6 = (bf16[8,128,128]{2,1,0:T(8,128)(2,1)S(1)}, bf16[8,128,128]{2,1,0:T(8,128)(2,1)S(1)}, u32[]{:S(2)}, u32[]{:S(2)}) collective-permute-start(bf16[8,128,128]{2,1,0:T(8,128)(2,1)S(1)} %get-tuple-element.31), channel_id=1, source_target_pairs={{0,16},{1,113},{2,18},{3,115},{4,20},{5,117},{6,22},{7,119},{8,24}... | collective-permute-start | bytes 786440 | tf_op jit(solution)/shard_map/ppermute | solution.py:150
  137.0 12.6 %collective-permute-start.7 = (bf16[8,128,128]{2,1,0:T(8,128)(2,1)S(1)}, bf16[8,128,128]{2,1,0:T(8,128)(2,1)S(1)}, u32[]{:S(2)}, u32[]{:S(2)}) collective-permute-start(bf16[8,128,128]{2,1,0:T(8,128)(2,1)S(1)} %get-tuple-element.32), channel_id=1, source_target_pairs={{0,8},{1,121},{2,10},{3,123},{4,12},{5,125},{6,14},{7,127},{8,16},... | collective-permute-start | bytes 786440 | tf_op jit(solution)/shard_map/ppermute | solution.py:150
  139.0 6.4 %collective-permute-start.13 = (bf16[5,128,128]{2,1,0:T(8,128)(2,1)S(1)}, bf16[5,128,128]{2,1,0:T(8,128)(2,1)S(1)}, u32[]{:S(2)}, u32[]{:S(2)}) collective-permute-start(bf16[5,128,128]{2,1,0:T(8,128)(2,1)S(1)} %get-tuple-element.39), channel_id=1, source_target_pairs={{0,384},{1,385},{2,386},{3,387},{4,388},{5,389},{6,390},{7,391},{8... | collective-permute-start | bytes 491528 | tf_op jit(solution)/shard_map/ppermute | solution.py:150
  150.6 5.4 %collective-permute-start.19 = (f32[512,128]{1,0:T(8,128)S(1)}, f32[512,128]{1,0:T(8,128)S(1)}, u32[]{:S(2)}, u32[]{:S(2)}) collective-permute-start(f32[512,128]{1,0:T(8,128)S(1)} %bitcast.22), channel_id=1, source_target_pairs={{0,1},{1,0},{2,3},{3,2},{4,5},{5,4},{6,7},{7,6},{8,9},{9,8},{10,11... | collective-permute-start | bytes 786440 | tf_op jit(solution)/shard_map/ppermute | solution.py:116
  154.8 18.7 %copy-start.4 = (f32[1,512]{1,0:T(1,128)S(1)}, f32[1,512]{1,0:T(1,128)}, u32[]{:S(2)}) copy-start(f32[1,512]{1,0:T(1,128)} %param.7) | copy-start | bytes 6148
  154.8 19.3 %copy-start.3 = (f32[1,512,128]{2,1,0:T(8,128)S(1)}, f32[1,512,128]{2,1,0:T(8,128)}, u32[]{:S(2)}) copy-start(f32[1,512,128]{2,1,0:T(8,128)} %param.6) | copy-start | bytes 786436
  168.7 4.7 %collective-permute-start.20 = (f32[256,128]{1,0:T(8,128)S(1)}, f32[256,128]{1,0:T(8,128)S(1)}, u32[]{:S(2)}, u32[]{:S(2)}) collective-permute-start(f32[256,128]{1,0:T(8,128)S(1)} %reduce_sum.18), channel_id=1, source_target_pairs={{0,1},{1,0},{2,3},{3,2},{4,5},{5,4},{6,7},{7,6},{8,9},{9,8},{10,11... | collective-permute-start | bytes 393224 | tf_op jit(solution)/shard_map/ppermute | solution.py:125

commit v4 on v3

--- a/solution.py
+++ b/solution.py
@@ -11,8 +11,8 @@
 X = 4
 Z = 16
 HALF = Z // 2
-NEAR = (1, 2, 3)
-FAR = ((8, 7, 6), (5, 4))
+NEAR = (1, 2, 3, 4)
+FAR = (8, 7, 6, 5)
 
 
 def vmem_specs(n):
@@ -21,16 +21,27 @@
 
 SMEM = pl.BlockSpec(memory_space=pltpu.SMEM)
 PARAMS = pltpu.CompilerParams(vmem_limit_bytes=16 << 20)
+
+
+def in_hbm(value):
+    return pltpu.with_memory_space_constraint(value, pltpu.HBM)
 
 
 def relayout(src, row_ids, local):
     samples, tables, width = local.shape
     others = (HALF - 1) * X
 
-    def kernel(src_ref, rows_ref, in_ref, table_ref, half_ref, other_ref):
+    def kernel(src_ref, rows_hbm, in_hbm, table_ref, half_ref, other_ref, rows_ref, in_ref, sems):
+        copies = [pltpu.make_async_copy(rows_hbm, rows_ref, sems.at[X])]
         for g in range(X):
-            block = jnp.swapaxes(in_ref[:, g * Z : (g + 1) * Z, :], 0, 1)
-            table_ref[g * Z : (g + 1) * Z] = block
+            part = in_hbm.at[:, g * Z : (g + 1) * Z, :]
+            copies.append(pltpu.make_async_copy(part, in_ref.at[g], sems.at[g]))
+        for copy in copies:
+            copy.start()
+        copies[0].wait()
+        for g in range(X):
+            copies[1 + g].wait()
+            table_ref[g * Z : (g + 1) * Z] = jnp.swapaxes(in_ref[g], 0, 1)
         for j in range(X):
             half_ref[j] = table_ref[src_ref[HALF * X + j]]
         for n in range(others):
@@ -46,18 +57,23 @@
     return pl.pallas_call(
         kernel,
         out_shape=[out(tables), out(X), out(others + 1)],
-        in_specs=[SMEM] + vmem_specs(2),
+        in_specs=[SMEM] + [pl.BlockSpec(memory_space=pltpu.HBM)] * 2,
         out_specs=vmem_specs(3),
+        scratch_shapes=[
+            pltpu.VMEM((1, row_ids.shape[0]), row_ids.dtype),
+            pltpu.VMEM((X, samples, Z, width), local.dtype),
+            pltpu.SemaphoreType.DMA((X + 1,)),
+        ],
         compiler_params=PARAMS,
         name="relayout",
-    )(src, row_ids[None], local)
-
-
-def regroup(src, inputs, plans):
+    )(src, in_hbm(row_ids[None]), in_hbm(local))
+
+
+def regroup(src, inputs, plans, after=()):
     block = inputs[0].shape[1:]
 
     def kernel(src_ref, *refs):
-        in_refs, out_refs = refs[: len(inputs)], refs[len(inputs) :]
+        in_refs, out_refs = refs[: len(inputs)], refs[len(inputs) + len(after) :]
         for out_ref, plan in zip(out_refs, plans):
             for n, (i, k, *place) in enumerate(plan):
                 out_ref[n] = in_refs[i][src_ref[place[0]] if k is None else k]
@@ -65,11 +81,11 @@
     return pl.pallas_call(
         kernel,
         out_shape=[jax.ShapeDtypeStruct((len(p),) + block, inputs[0].dtype) for p in plans],
-        in_specs=[SMEM] + vmem_specs(len(inputs)),
+        in_specs=[SMEM] + vmem_specs(len(inputs)) + [pl.BlockSpec(memory_space=pl.ANY)] * len(after),
         out_specs=vmem_specs(len(plans)),
         compiler_params=PARAMS,
         name="regroup",
-    )(src, *inputs)
+    )(src, *inputs, *after)
 
 
 def add_tiles(partial, groups, tile, mult, rows, row_blocks):
@@ -180,29 +196,27 @@
     def both(i, j):
         return [(0, None, i * X + j), (1, (i - 1) * X + j)]
 
-    far_shifts = (7, 6, 5, 4)
+    far_shifts = FAR[1:]
     plans = [[both(i, j)[s] for s in range(2) for j in range(X)] for i in far_shifts]
     plans += [[(0, None, j)] + [b for i in NEAR for b in both(i, j)] for j in range(X)]
     made = regroup(src, [by_table, sib], plans)
     mine, near = dict(zip(far_shifts, made)), list(made[len(far_shifts) :])
-    for i in (7, 6):
+    for i in far_shifts:
         got[i] = move(mine[i], over_z(i))
     for j in range(1, X):
         near[j] = move(near[j], over_x(j))
-    for i in (5, 4):
-        got[i] = move(mine[i], over_z(i))
     mult = (mult, move(mult, other_core))
 
     def far(shifts):
         who = [(n, i, s) for n, i in enumerate(shifts) for s in range(1 if i == HALF else 2)]
         plans = [[(n, s * X + j) for n, _, s in who] for j in range(X)]
-        made = list(regroup(src, [got[i] for i in shifts], plans))
+        made = list(regroup(src, [got[i] for i in shifts], plans, mult[1:]))
         for j in range(1, X):
             made[j] = move(made[j], over_x(j))
         return [(made[j], [(i, j, s) for _, i, s in who]) for j in range(X)]
 
     groups = [(near[j], [(0, j, 0)]) for j in range(X)]
-    groups += far(FAR[0])
+    groups += far(FAR)
     plans = [
         [(j, 1 + 2 * NEAR.index(i) + s) for s in range(2) for j in range(X)] for i in NEAR
     ]
@@ -211,7 +225,6 @@
     for i in NEAR[::-1]:
         blocks = move(made[NEAR.index(i)], over_z(i))
         last.append((blocks, [(i, j, s) for s in range(2) for j in range(X)]))
-    groups += far(FAR[1])
     partial = add_tiles(None, groups, tile, mult, rows, row_blocks)
     return add_tiles(partial, last, tile, mult, rows, row_blocks)
 

time: 176 us -> 164 us (0.932); the launches traced: 175 us -> 161 us
  starting transfers between devices: 120 us -> 100 us
  waiting for transfers between devices: 31.4 us -> 38.6 us
  local copies, waits for them, and re-layouts: 2.31 us -> 0.08 us
    ppermute x19 -> x16, starting transfers between devices: 112 us -> 93.8 us  [move(): return lax.ppermute(value, ('mp', 'replica'), pairs(shift))]
    ppermute x19 -> x16, waiting for transfers between devices: 29.3 us -> 36.5 us  [move(): return lax.ppermute(value, ('mp', 'replica'), pairs(shift))]
    unnamed x10 -> x8, local copies, waits for them, and re-layouts: 2.26 us -> 0.03 us
  transfers between devices with their start and end apart: 21 -> 18, of which waited for: 7 -> 7; matrix products, arithmetic and copies ran while one was open for 0% -> 0% of each run, Pallas kernels for 3% -> 3%
where the time goes in v4:
time: 164 us; the launch traced here: 161 us
  starting transfers between devices  100 us (61%)
  waiting for transfers between devices  38.6 us (24%)
  blocking collectives  12.6 us (8%)
  Pallas kernels  6.45 us (4%)
  other arithmetic  1.69 us (1%)
    ppermute x16, starting transfers between devices, move(): return lax.ppermute(value, ('mp', 'replica'), pairs(shift))  93.8 us
    ppermute x16, waiting for transfers between devices, move(): return lax.ppermute(value, ('mp', 'replica'), pairs(shift))  36.5 us
    all_to_all x1, blocking collectives, sum_over_replicas(): lax.all_to_all(copies, 'replica', split_axis=0, concat_axis=0, axis_index...  12.6 us
    ppermute x1, starting transfers between devices, sum_over_replicas(): other = lax.ppermute(own, 'replica', swap)  3.71 us
  transfers between devices with their start and end apart: 18, of which 7 were waited for; matrix products, arithmetic and copies ran while one was open for 0% of the time, Pallas kernels for 3%

profile of v4, /device:TPU:1, one launch (start us, length us, event | category | flops | bytes accessed | tf_op | source)
XLA Modules:
  0.0 160.7 jit_solution(3501137841642557921)
XLA Ops:
  0.6 8.7 %collective-permute-start.1 = (bf16[64,128,128]{2,1,0:T(8,128)(2,1)}, bf16[64,128,128]{2,1,0:T(8,128)(2,1)S(1)}, u32[]{:S(2)}, u32[]{:S(2)}) collective-permute-start(bf16[64,128,128]{2,1,0:T(8,128)(2,1)} %bitcast.18), channel_id=1, source_target_pairs={{0,1},{1,0},{2,3},{3,2},{4,5},{5,4},{6,7},{7,6},{8,9},{9,8},{10,11... | collective-permute-start | bytes 6291464 | tf_op jit(solution)/shard_map/ppermute | solution.py:166
  9.4 2.4 %relayout.1 = (bf16[64,128,128]{2,1,0:T(8,128)(2,1)S(1)}, bf16[4,128,128]{2,1,0:T(8,128)(2,1)S(1)}, bf16[29,128,128]{2,1,0:T(8,128)(2,1)S(1)}) custom-call(s32[64]{0:T(128)S(1)} %fusion.4.src_ref, s32[1,64]{1,0:T(1,128)} %bitcast.22, bf16[128,64,128]{2,1,0:T(8,128)(2,1)} %bitcast.25), custom_call_target="tpu_custom_call" | custom-call | tf_op jit(solution)/shard_map/relayout/pallas_call | solution.py:57
  11.9 1.9 %collective-permute-start = (bf16[29,128,128]{2,1,0:T(8,128)(2,1)S(1)}, bf16[29,128,128]{2,1,0:T(8,128)(2,1)S(1)}, u32[]{:S(2)}, u32[]{:S(2)}) collective-permute-start(bf16[29,128,128]{2,1,0:T(8,128)(2,1)S(1)} %get-tuple-element.20), channel_id=1, source_target_pairs={{0,1},{1,0},{2,3},{3,2},{4,5},{5,4},{6,7},{7,6},{8,9},{9,8},{10,11... | collective-permute-start | bytes 2850824 | tf_op jit(solution)/shard_map/ppermute | solution.py:166
  13.8 2.5 %collective-permute-done.refs_1_ = bf16[29,128,128]{2,1,0:T(8,128)(2,1)S(1)} collective-permute-done((bf16[29,128,128]{2,1,0:T(8,128)(2,1)S(1)}, bf16[29,128,128]{2,1,0:T(8,128)(2,1)S(1)}, u32[]{:S(2)}, u32[]{:S(2)}) %collective-permute-start) | collective-permute-done | bytes 950304 | tf_op jit(solution)/shard_map/ppermute | solution.py:166
  16.3 0.7 regroup.3
  17.0 9.7 %collective-permute-start.10 = (bf16[8,128,128]{2,1,0:T(8,128)(2,1)S(1)}, bf16[8,128,128]{2,1,0:T(8,128)(2,1)S(1)}, u32[]{:S(2)}, u32[]{:S(2)}) collective-permute-start(bf16[8,128,128]{2,1,0:T(8,128)(2,1)S(1)} %get-tuple-element.31), channel_id=1, source_target_pairs={{0,56},{1,73},{2,58},{3,75},{4,60},{5,77},{6,62},{7,79},{8,64},{9,... | collective-permute-start | bytes 786440 | tf_op jit(solution)/shard_map/ppermute | solution.py:166
  26.6 1.9 %collective-permute-start.11 = (bf16[8,128,128]{2,1,0:T(8,128)(2,1)S(1)}, bf16[8,128,128]{2,1,0:T(8,128)(2,1)S(1)}, u32[]{:S(2)}, u32[]{:S(2)}) collective-permute-start(bf16[8,128,128]{2,1,0:T(8,128)(2,1)S(1)} %get-tuple-element.32), channel_id=1, source_target_pairs={{0,48},{1,81},{2,50},{3,83},{4,52},{5,85},{6,54},{7,87},{8,56},{9,... | collective-permute-start | bytes 786440 | tf_op jit(solution)/shard_map/ppermute | solution.py:166
  28.6 8.6 %collective-permute-start.12 = (bf16[8,128,128]{2,1,0:T(8,128)(2,1)S(1)}, bf16[8,128,128]{2,1,0:T(8,128)(2,1)S(1)}, u32[]{:S(2)}, u32[]{:S(2)}) collective-permute-start(bf16[8,128,128]{2,1,0:T(8,128)(2,1)S(1)} %get-tuple-element.33), channel_id=1, source_target_pairs={{0,40},{1,89},{2,42},{3,91},{4,44},{5,93},{6,46},{7,95},{8,48},{9,... | collective-permute-start | bytes 786440 | tf_op jit(solution)/shard_map/ppermute | solution.py:166
  37.2 5.2 %collective-permute-start.9 = (bf16[4,128,128]{2,1,0:T(8,128)(2,1)S(1)}, bf16[4,128,128]{2,1,0:T(8,128)(2,1)S(1)}, u32[]{:S(2)}, u32[]{:S(2)}) collective-permute-start(bf16[4,128,128]{2,1,0:T(8,128)(2,1)S(1)} %get-tuple-element.30), channel_id=1, source_target_pairs={{0,64},{1,65},{2,66},{3,67},{4,68},{5,69},{6,70},{7,71},{8,72},{9,... | collective-permute-start | bytes 393224 | tf_op jit(solution)/shard_map/ppermute | solution.py:166
  42.4 25.8 %collective-permute-done.9.refs_0_ = bf16[4,128,128]{2,1,0:T(8,128)(2,1)S(1)} collective-permute-done((bf16[4,128,128]{2,1,0:T(8,128)(2,1)S(1)}, bf16[4,128,128]{2,1,0:T(8,128)(2,1)S(1)}, u32[]{:S(2)}, u32[]{:S(2)}) %collective-permute-start.9) | collective-permute-done | bytes 131104 | tf_op jit(solution)/shard_map/ppermute | solution.py:166
  68.2 2.4 %collective-permute-start.2 = (bf16[9,128,128]{2,1,0:T(8,128)(2,1)S(1)}, bf16[9,128,128]{2,1,0:T(8,128)(2,1)S(1)}, u32[]{:S(2)}, u32[]{:S(2)}) collective-permute-start(bf16[9,128,128]{2,1,0:T(8,128)(2,1)S(1)} %get-tuple-element.23), channel_id=1, source_target_pairs={{0,128},{1,129},{2,130},{3,131},{4,132},{5,133},{6,134},{7,135},{8... | collective-permute-start | bytes 884744 | tf_op jit(solution)/shard_map/ppermute | solution.py:166
  70.5 0.0 collective-permute-done.10.refs_1_
  70.6 4.4 %collective-permute-start.3 = (bf16[9,128,128]{2,1,0:T(8,128)(2,1)S(1)}, bf16[9,128,128]{2,1,0:T(8,128)(2,1)S(1)}, u32[]{:S(2)}, u32[]{:S(2)}) collective-permute-start(bf16[9,128,128]{2,1,0:T(8,128)(2,1)S(1)} %get-tuple-element.24), channel_id=1, source_target_pairs={{0,256},{1,257},{2,258},{3,259},{4,260},{5,261},{6,262},{7,263},{8... | collective-permute-start | bytes 884744 | tf_op jit(solution)/shard_map/ppermute | solution.py:166
  74.9 0.0 copy-start
  74.9 0.0 copy-start.1
  75.0 10.7 %collective-permute-start.4 = (bf16[9,128,128]{2,1,0:T(8,128)(2,1)S(1)}, bf16[9,128,128]{2,1,0:T(8,128)(2,1)S(1)}, u32[]{:S(2)}, u32[]{:S(2)}) collective-permute-start(bf16[9,128,128]{2,1,0:T(8,128)(2,1)S(1)} %get-tuple-element.25), channel_id=1, source_target_pairs={{0,384},{1,385},{2,386},{3,387},{4,388},{5,389},{6,390},{7,391},{8... | collective-permute-start | bytes 884744 | tf_op jit(solution)/shard_map/ppermute | solution.py:166
  85.7 0.0 collective-permute-done.12.refs_3_
  85.7 0.0 collective-permute-done.1.refs_4_.mult1
  85.7 0.6 regroup.5
  86.3 6.5 %collective-permute-start.13 = (bf16[7,128,128]{2,1,0:T(8,128)(2,1)S(1)}, bf16[7,128,128]{2,1,0:T(8,128)(2,1)S(1)}, u32[]{:S(2)}, u32[]{:S(2)}) collective-permute-start(bf16[7,128,128]{2,1,0:T(8,128)(2,1)S(1)} %get-tuple-element.35), channel_id=1, source_target_pairs={{0,128},{1,129},{2,130},{3,131},{4,132},{5,133},{6,134},{7,135},{8... | collective-permute-start | bytes 688136 | tf_op jit(solution)/shard_map/ppermute | solution.py:166
  92.8 4.4 %collective-permute-start.14 = (bf16[7,128,128]{2,1,0:T(8,128)(2,1)S(1)}, bf16[7,128,128]{2,1,0:T(8,128)(2,1)S(1)}, u32[]{:S(2)}, u32[]{:S(2)}) collective-permute-start(bf16[7,128,128]{2,1,0:T(8,128)(2,1)S(1)} %get-tuple-element.36), channel_id=1, source_target_pairs={{0,256},{1,257},{2,258},{3,259},{4,260},{5,261},{6,262},{7,263},{8... | collective-permute-start | bytes 688136 | tf_op jit(solution)/shard_map/ppermute | solution.py:166
  97.2 0.0 collective-permute-done.2.refs_1_
  97.2 0.0 collective-permute-done.3.refs_2_
  97.2 0.6 regroup.4
  97.8 4.1 %collective-permute-start.5 = (bf16[8,128,128]{2,1,0:T(8,128)(2,1)S(1)}, bf16[8,128,128]{2,1,0:T(8,128)(2,1)S(1)}, u32[]{:S(2)}, u32[]{:S(2)}) collective-permute-start(bf16[8,128,128]{2,1,0:T(8,128)(2,1)S(1)} %get-tuple-element.26), channel_id=1, source_target_pairs={{0,32},{1,97},{2,34},{3,99},{4,36},{5,101},{6,38},{7,103},{8,40},{... | collective-permute-start | bytes 786440 | tf_op jit(solution)/shard_map/ppermute | solution.py:166
  102.0 17.3 %collective-permute-start.6 = (bf16[8,128,128]{2,1,0:T(8,128)(2,1)S(1)}, bf16[8,128,128]{2,1,0:T(8,128)(2,1)S(1)}, u32[]{:S(2)}, u32[]{:S(2)}) collective-permute-start(bf16[8,128,128]{2,1,0:T(8,128)(2,1)S(1)} %get-tuple-element.27), channel_id=1, source_target_pairs={{0,24},{1,105},{2,26},{3,107},{4,28},{5,109},{6,30},{7,111},{8,32}... | collective-permute-start | bytes 786440 | tf_op jit(solution)/shard_map/ppermute | solution.py:166
  119.2 1.9 %collective-permute-start.7 = (bf16[8,128,128]{2,1,0:T(8,128)(2,1)S(1)}, bf16[8,128,128]{2,1,0:T(8,128)(2,1)S(1)}, u32[]{:S(2)}, u32[]{:S(2)}) collective-permute-start(bf16[8,128,128]{2,1,0:T(8,128)(2,1)S(1)} %get-tuple-element.28), channel_id=1, source_target_pairs={{0,16},{1,113},{2,18},{3,115},{4,20},{5,117},{6,22},{7,119},{8,24}... | collective-permute-start | bytes 786440 | tf_op jit(solution)/shard_map/ppermute | solution.py:166
  121.2 0.0 collective-permute-done.13.refs_5_
  121.2 2.2 %collective-permute-start.8 = (bf16[8,128,128]{2,1,0:T(8,128)(2,1)S(1)}, bf16[8,128,128]{2,1,0:T(8,128)(2,1)S(1)}, u32[]{:S(2)}, u32[]{:S(2)}) collective-permute-start(bf16[8,128,128]{2,1,0:T(8,128)(2,1)S(1)} %get-tuple-element.29), channel_id=1, source_target_pairs={{0,8},{1,121},{2,10},{3,123},{4,12},{5,125},{6,14},{7,127},{8,16},... | collective-permute-start | bytes 786440 | tf_op jit(solution)/shard_map/ppermute | solution.py:166
  123.4 0.0 collective-permute-done.14.refs_6_
  123.4 4.0 %collective-permute-start.15 = (bf16[7,128,128]{2,1,0:T(8,128)(2,1)S(1)}, bf16[7,128,128]{2,1,0:T(8,128)(2,1)S(1)}, u32[]{:S(2)}, u32[]{:S(2)}) collective-permute-start(bf16[7,128,128]{2,1,0:T(8,128)(2,1)S(1)} %get-tuple-element.37), channel_id=1, source_target_pairs={{0,384},{1,385},{2,386},{3,387},{4,388},{5,389},{6,390},{7,391},{8... | collective-permute-start | bytes 688136 | tf_op jit(solution)/shard_map/ppermute | solution.py:166
  127.4 3.1 %collective-permute-done.15.refs_7_ = bf16[7,128,128]{2,1,0:T(8,128)(2,1)S(1)} collective-permute-done((bf16[7,128,128]{2,1,0:T(8,128)(2,1)S(1)}, bf16[7,128,128]{2,1,0:T(8,128)(2,1)S(1)}, u32[]{:S(2)}, u32[]{:S(2)}) %collective-permute-start.15) | collective-permute-done | bytes 229408 | tf_op jit(solution)/shard_map/ppermute | solution.py:166
  130.4 1.1 add_tiles.2.refs_4_
  131.5 0.0 collective-permute-done.5.refs_0_
  131.5 0.0 collective-permute-done.6.refs_1_
  131.5 2.3 %collective-permute-done.7.refs_2_ = bf16[8,128,128]{2,1,0:T(8,128)(2,1)S(1)} collective-permute-done((bf16[8,128,128]{2,1,0:T(8,128)(2,1)S(1)}, bf16[8,128,128]{2,1,0:T(8,128)(2,1)S(1)}, u32[]{:S(2)}, u32[]{:S(2)}) %collective-permute-start.7) | collective-permute-done | bytes 262176 | tf_op jit(solution)/shard_map/ppermute | solution.py:166
  133.9 2.8 %collective-permute-done.8.refs_3_ = bf16[8,128,128]{2,1,0:T(8,128)(2,1)S(1)} collective-permute-done((bf16[8,128,128]{2,1,0:T(8,128)(2,1)S(1)}, bf16[8,128,128]{2,1,0:T(8,128)(2,1)S(1)}, u32[]{:S(2)}, u32[]{:S(2)}) %collective-permute-start.8) | collective-permute-done | bytes 262176 | tf_op jit(solution)/shard_map/ppermute | solution.py:166
  136.7 1.1 add_tiles.3
  137.7 2.7 %collective-permute-start.16 = (f32[512,128]{1,0:T(8,128)S(1)}, f32[512,128]{1,0:T(8,128)S(1)}, u32[]{:S(2)}, u32[]{:S(2)}) collective-permute-start(f32[512,128]{1,0:T(8,128)S(1)} %bitcast.21), channel_id=1, source_target_pairs={{0,1},{1,0},{2,3},{3,2},{4,5},{5,4},{6,7},{7,6},{8,9},{9,8},{10,11... | collective-permute-start | bytes 786440 | tf_op jit(solution)/shard_map/ppermute | solution.py:132
  140.5 0.0 copy-start.3
  140.5 0.0 copy-start.2
  140.5 1.1 collective-permute-done.16
  141.7 12.6 %all_to_all.5 = f32[4,256,128]{2,1,0:T(8,128)S(1)} all-to-all(f32[4,256,128]{2,1,0:T(8,128)S(1)} %broadcast_in_dim.5), channel_id=1, replica_groups={{0,2,4,6},{1,3,5,7},{8,10,12,14},{9,11,13,15},{16,18,20,22},{17,19,21,2..., dimensions={0} | all-to-all | bytes 1048576 | tf_op jit(solution)/shard_map/all_to_all | solution.py:137
  154.3 3.7 %collective-permute-start.17 = (f32[256,128]{1,0:T(8,128)S(1)}, f32[256,128]{1,0:T(8,128)S(1)}, u32[]{:S(2)}, u32[]{:S(2)}) collective-permute-start(f32[256,128]{1,0:T(8,128)S(1)} %reduce_sum.18), channel_id=1, source_target_pairs={{0,1},{1,0},{2,3},{3,2},{4,5},{5,4},{6,7},{7,6},{8,9},{9,8},{10,11... | collective-permute-start | bytes 393224 | tf_op jit(solution)/shard_map/ppermute | solution.py:141
  158.1 1.0 collective-permute-done.17
  159.0 0.1 fusion.2
  159.2 0.6 add.92
  159.8 0.8 fusion.1
  (15 shorter events, 0.2 us)
Async XLA Ops:
  0.6 85.1 %collective-permute-start.1 = (bf16[64,128,128]{2,1,0:T(8,128)(2,1)}, bf16[64,128,128]{2,1,0:T(8,128)(2,1)S(1)}, u32[]{:S(2)}, u32[]{:S(2)}) collective-permute-start(bf16[64,128,128]{2,1,0:T(8,128)(2,1)} %bitcast.18), channel_id=1, source_target_pairs={{0,1},{1,0},{2,3},{3,2},{4,5},{5,4},{6,7},{7,6},{8,9},{9,8},{10,11... | collective-permute-start | bytes 6291464 | tf_op jit(solution)/shard_map/ppermute | solution.py:166
  11.9 4.4 %collective-permute-start = (bf16[29,128,128]{2,1,0:T(8,128)(2,1)S(1)}, bf16[29,128,128]{2,1,0:T(8,128)(2,1)S(1)}, u32[]{:S(2)}, u32[]{:S(2)}) collective-permute-start(bf16[29,128,128]{2,1,0:T(8,128)(2,1)S(1)} %get-tuple-element.20), channel_id=1, source_target_pairs={{0,1},{1,0},{2,3},{3,2},{4,5},{5,4},{6,7},{7,6},{8,9},{9,8},{10,11... | collective-permute-start | bytes 2850824 | tf_op jit(solution)/shard_map/ppermute | solution.py:166
  17.0 53.6 %collective-permute-start.10 = (bf16[8,128,128]{2,1,0:T(8,128)(2,1)S(1)}, bf16[8,128,128]{2,1,0:T(8,128)(2,1)S(1)}, u32[]{:S(2)}, u32[]{:S(2)}) collective-permute-start(bf16[8,128,128]{2,1,0:T(8,128)(2,1)S(1)} %get-tuple-element.31), channel_id=1, source_target_pairs={{0,56},{1,73},{2,58},{3,75},{4,60},{5,77},{6,62},{7,79},{8,64},{9,... | collective-permute-start | bytes 786440 | tf_op jit(solution)/shard_map/ppermute | solution.py:166
  26.6 48.3 %collective-permute-start.11 = (bf16[8,128,128]{2,1,0:T(8,128)(2,1)S(1)}, bf16[8,128,128]{2,1,0:T(8,128)(2,1)S(1)}, u32[]{:S(2)}, u32[]{:S(2)}) collective-permute-start(bf16[8,128,128]{2,1,0:T(8,128)(2,1)S(1)} %get-tuple-element.32), channel_id=1, source_target_pairs={{0,48},{1,81},{2,50},{3,83},{4,52},{5,85},{6,54},{7,87},{8,56},{9,... | collective-permute-start | bytes 786440 | tf_op jit(solution)/shard_map/ppermute | solution.py:166
  28.6 57.1 %collective-permute-start.12 = (bf16[8,128,128]{2,1,0:T(8,128)(2,1)S(1)}, bf16[8,128,128]{2,1,0:T(8,128)(2,1)S(1)}, u32[]{:S(2)}, u32[]{:S(2)}) collective-permute-start(bf16[8,128,128]{2,1,0:T(8,128)(2,1)S(1)} %get-tuple-element.33), channel_id=1, source_target_pairs={{0,40},{1,89},{2,42},{3,91},{4,44},{5,93},{6,46},{7,95},{8,48},{9,... | collective-permute-start | bytes 786440 | tf_op jit(solution)/shard_map/ppermute | solution.py:166
  37.2 30.9 %collective-permute-start.9 = (bf16[4,128,128]{2,1,0:T(8,128)(2,1)S(1)}, bf16[4,128,128]{2,1,0:T(8,128)(2,1)S(1)}, u32[]{:S(2)}, u32[]{:S(2)}) collective-permute-start(bf16[4,128,128]{2,1,0:T(8,128)(2,1)S(1)} %get-tuple-element.30), channel_id=1, source_target_pairs={{0,64},{1,65},{2,66},{3,67},{4,68},{5,69},{6,70},{7,71},{8,72},{9,... | collective-permute-start | bytes 393224 | tf_op jit(solution)/shard_map/ppermute | solution.py:166
  68.2 29.0 %collective-permute-start.2 = (bf16[9,128,128]{2,1,0:T(8,128)(2,1)S(1)}, bf16[9,128,128]{2,1,0:T(8,128)(2,1)S(1)}, u32[]{:S(2)}, u32[]{:S(2)}) collective-permute-start(bf16[9,128,128]{2,1,0:T(8,128)(2,1)S(1)} %get-tuple-element.23), channel_id=1, source_target_pairs={{0,128},{1,129},{2,130},{3,131},{4,132},{5,133},{6,134},{7,135},{8... | collective-permute-start | bytes 884744 | tf_op jit(solution)/shard_map/ppermute | solution.py:166
  70.6 26.6 %collective-permute-start.3 = (bf16[9,128,128]{2,1,0:T(8,128)(2,1)S(1)}, bf16[9,128,128]{2,1,0:T(8,128)(2,1)S(1)}, u32[]{:S(2)}, u32[]{:S(2)}) collective-permute-start(bf16[9,128,128]{2,1,0:T(8,128)(2,1)S(1)} %get-tuple-element.24), channel_id=1, source_target_pairs={{0,256},{1,257},{2,258},{3,259},{4,260},{5,261},{6,262},{7,263},{8... | collective-permute-start | bytes 884744 | tf_op jit(solution)/shard_map/ppermute | solution.py:166
  74.9 55.5 %copy-start = (bf16[1,1,64,128,128]{4,3,2,1,0:T(8,128)(2,1)S(1)}, bf16[1,1,64,128,128]{4,3,2,1,0:T(8,128)(2,1)}, u32[]{:S(2)}) copy-start(bf16[1,1,64,128,128]{4,3,2,1,0:T(8,128)(2,1)} %param.8) | copy-start | bytes 6291460
  74.9 55.5 %copy-start.1 = (s32[1,1,64]{2,1,0:T(1,128)S(1)}, s32[1,1,64]{2,1,0:T(1,128)}, u32[]{:S(2)}) copy-start(s32[1,1,64]{2,1,0:T(1,128)} %param.9) | copy-start | bytes 772
  75.0 22.2 %collective-permute-start.4 = (bf16[9,128,128]{2,1,0:T(8,128)(2,1)S(1)}, bf16[9,128,128]{2,1,0:T(8,128)(2,1)S(1)}, u32[]{:S(2)}, u32[]{:S(2)}) collective-permute-start(bf16[9,128,128]{2,1,0:T(8,128)(2,1)S(1)} %get-tuple-element.25), channel_id=1, source_target_pairs={{0,384},{1,385},{2,386},{3,387},{4,388},{5,389},{6,390},{7,391},{8... | collective-permute-start | bytes 884744 | tf_op jit(solution)/shard_map/ppermute | solution.py:166
  86.3 34.8 %collective-permute-start.13 = (bf16[7,128,128]{2,1,0:T(8,128)(2,1)S(1)}, bf16[7,128,128]{2,1,0:T(8,128)(2,1)S(1)}, u32[]{:S(2)}, u32[]{:S(2)}) collective-permute-start(bf16[7,128,128]{2,1,0:T(8,128)(2,1)S(1)} %get-tuple-element.35), channel_id=1, source_target_pairs={{0,128},{1,129},{2,130},{3,131},{4,132},{5,133},{6,134},{7,135},{8... | collective-permute-start | bytes 688136 | tf_op jit(solution)/shard_map/ppermute | solution.py:166
  92.8 30.6 %collective-permute-start.14 = (bf16[7,128,128]{2,1,0:T(8,128)(2,1)S(1)}, bf16[7,128,128]{2,1,0:T(8,128)(2,1)S(1)}, u32[]{:S(2)}, u32[]{:S(2)}) collective-permute-start(bf16[7,128,128]{2,1,0:T(8,128)(2,1)S(1)} %get-tuple-element.36), channel_id=1, source_target_pairs={{0,256},{1,257},{2,258},{3,259},{4,260},{5,261},{6,262},{7,263},{8... | collective-permute-start | bytes 688136 | tf_op jit(solution)/shard_map/ppermute | solution.py:166
  97.8 33.7 %collective-permute-start.5 = (bf16[8,128,128]{2,1,0:T(8,128)(2,1)S(1)}, bf16[8,128,128]{2,1,0:T(8,128)(2,1)S(1)}, u32[]{:S(2)}, u32[]{:S(2)}) collective-permute-start(bf16[8,128,128]{2,1,0:T(8,128)(2,1)S(1)} %get-tuple-element.26), channel_id=1, source_target_pairs={{0,32},{1,97},{2,34},{3,99},{4,36},{5,101},{6,38},{7,103},{8,40},{... | collective-permute-start | bytes 786440 | tf_op jit(solution)/shard_map/ppermute | solution.py:166
  102.0 29.6 %collective-permute-start.6 = (bf16[8,128,128]{2,1,0:T(8,128)(2,1)S(1)}, bf16[8,128,128]{2,1,0:T(8,128)(2,1)S(1)}, u32[]{:S(2)}, u32[]{:S(2)}) collective-permute-start(bf16[8,128,128]{2,1,0:T(8,128)(2,1)S(1)} %get-tuple-element.27), channel_id=1, source_target_pairs={{0,24},{1,105},{2,26},{3,107},{4,28},{5,109},{6,30},{7,111},{8,32}... | collective-permute-start | bytes 786440 | tf_op jit(solution)/shard_map/ppermute | solution.py:166
  119.2 14.6 %collective-permute-start.7 = (bf16[8,128,128]{2,1,0:T(8,128)(2,1)S(1)}, bf16[8,128,128]{2,1,0:T(8,128)(2,1)S(1)}, u32[]{:S(2)}, u32[]{:S(2)}) collective-permute-start(bf16[8,128,128]{2,1,0:T(8,128)(2,1)S(1)} %get-tuple-element.28), channel_id=1, source_target_pairs={{0,16},{1,113},{2,18},{3,115},{4,20},{5,117},{6,22},{7,119},{8,24}... | collective-permute-start | bytes 786440 | tf_op jit(solution)/shard_map/ppermute | solution.py:166
  121.2 15.5 %collective-permute-start.8 = (bf16[8,128,128]{2,1,0:T(8,128)(2,1)S(1)}, bf16[8,128,128]{2,1,0:T(8,128)(2,1)S(1)}, u32[]{:S(2)}, u32[]{:S(2)}) collective-permute-start(bf16[8,128,128]{2,1,0:T(8,128)(2,1)S(1)} %get-tuple-element.29), channel_id=1, source_target_pairs={{0,8},{1,121},{2,10},{3,123},{4,12},{5,125},{6,14},{7,127},{8,16},... | collective-permute-start | bytes 786440 | tf_op jit(solution)/shard_map/ppermute | solution.py:166
  123.4 7.1 %collective-permute-start.15 = (bf16[7,128,128]{2,1,0:T(8,128)(2,1)S(1)}, bf16[7,128,128]{2,1,0:T(8,128)(2,1)S(1)}, u32[]{:S(2)}, u32[]{:S(2)}) collective-permute-start(bf16[7,128,128]{2,1,0:T(8,128)(2,1)S(1)} %get-tuple-element.37), channel_id=1, source_target_pairs={{0,384},{1,385},{2,386},{3,387},{4,388},{5,389},{6,390},{7,391},{8... | collective-permute-start | bytes 688136 | tf_op jit(solution)/shard_map/ppermute | solution.py:166
  137.7 3.9 %collective-permute-start.16 = (f32[512,128]{1,0:T(8,128)S(1)}, f32[512,128]{1,0:T(8,128)S(1)}, u32[]{:S(2)}, u32[]{:S(2)}) collective-permute-start(f32[512,128]{1,0:T(8,128)S(1)} %bitcast.21), channel_id=1, source_target_pairs={{0,1},{1,0},{2,3},{3,2},{4,5},{5,4},{6,7},{7,6},{8,9},{9,8},{10,11... | collective-permute-start | bytes 786440 | tf_op jit(solution)/shard_map/ppermute | solution.py:132
  140.5 18.7 %copy-start.3 = (f32[1,512]{1,0:T(1,128)S(1)}, f32[1,512]{1,0:T(1,128)}, u32[]{:S(2)}) copy-start(f32[1,512]{1,0:T(1,128)} %param.7) | copy-start | bytes 6148
  140.5 19.3 %copy-start.2 = (f32[1,512,128]{2,1,0:T(8,128)S(1)}, f32[1,512,128]{2,1,0:T(8,128)}, u32[]{:S(2)}) copy-start(f32[1,512,128]{2,1,0:T(8,128)} %param.6) | copy-start | bytes 786436
  154.3 4.7 %collective-permute-start.17 = (f32[256,128]{1,0:T(8,128)S(1)}, f32[256,128]{1,0:T(8,128)S(1)}, u32[]{:S(2)}, u32[]{:S(2)}) collective-permute-start(f32[256,128]{1,0:T(8,128)S(1)} %reduce_sum.18), channel_id=1, source_target_pairs={{0,1},{1,0},{2,3},{3,2},{4,5},{5,4},{6,7},{7,6},{8,9},{9,8},{10,11... | collective-permute-start | bytes 393224 | tf_op jit(solution)/shard_map/ppermute | solution.py:141

commit v5 on v4

--- a/solution.py
+++ b/solution.py
@@ -88,22 +88,22 @@
     )(src, *inputs, *after)
 
 
-def add_tiles(partial, groups, tile, mult, rows, row_blocks):
+def add_tiles(partial, groups, ids, mult, row_blocks):
     blocks = [g for g, _ in groups]
     pairs_of = [p for _, ps in groups for p in ps]
     owner = [(n, k) for n, (_, ps) in enumerate(groups) for k in range(len(ps))]
     block, width = blocks[0].shape[1:]
 
-    def kernel(tile_ref, rows0, rows1, mult0, mult1, *refs):
+    def kernel(ids_ref, mult0, mult1, *refs):
         block_refs, out_ref = refs[: len(blocks)], refs[-1]
         if partial is None:
             out_ref[...] = jnp.zeros(out_ref.shape, out_ref.dtype)
         else:
             out_ref[...] = refs[-2][...]
         for (i, j, s), (g, k) in zip(pairs_of, owner):
-            t = tile_ref[i * X + j]
-            mult_ref, rows_ref = (mult1, rows1) if s else (mult0, rows0)
-            out_ref[rows_ref[t]] += lax.dot_general(
+            t = ids_ref[i * X + j]
+            mult_ref = mult1 if s else mult0
+            out_ref[ids_ref[(1 + s) * X * Z + t]] += lax.dot_general(
                 mult_ref[t],
                 block_refs[g][k],
                 (((0,), (0,)), ((), ())),
@@ -114,11 +114,11 @@
     return pl.pallas_call(
         kernel,
         out_shape=jax.ShapeDtypeStruct((row_blocks, block, width), jnp.float32),
-        in_specs=[SMEM] * 3 + vmem_specs(2 + len(blocks) + len(start)),
+        in_specs=[SMEM] + vmem_specs(2 + len(blocks) + len(start)),
         out_specs=vmem_specs(1)[0],
         compiler_params=PARAMS,
         name="add_tiles",
-    )(tile, *rows, *mult, *blocks, *start)
+    )(ids, *mult, *blocks, *start)
 
 
 def sum_over_replicas(partial_grad):
@@ -139,14 +139,37 @@
     )
     own = jnp.sum(shares, axis=0)
     other = lax.ppermute(own, "replica", swap)
-    first = core == 0
-    return jnp.concatenate([jnp.where(first, own, other), jnp.where(first, other, own)])
-
-
-def adagrad(weights_in, accum_in, gradient):
-    accum_out = accum_in + jnp.mean(gradient * gradient, axis=-1)
-    weights_out = weights_in - LEARN_RATE * gradient / (jnp.sqrt(accum_out)[..., None] + EPSILON)
-    return (weights_out, accum_out)
+    return core, own, other
+
+
+def update(core, own, other, weights_in, accum_in):
+    rows, width = weights_in.shape
+    half = rows // CORES
+
+    def kernel(core_ref, own_ref, other_ref, weights_ref, accum_ref, weights_out, accum_out):
+        first = core_ref[0] == 0
+        for at in range(0, rows, width):
+            part = slice(at % half, at % half + width)
+            one, two = own_ref[part], other_ref[part]
+            grad = jnp.where(first, one, two) if at < half else jnp.where(first, two, one)
+            square = jnp.mean(grad * grad, axis=-1, keepdims=True)
+            before = jnp.broadcast_to(accum_ref[:, at : at + width], (width, width)).T
+            accum = before + square
+            rate = LEARN_RATE * grad / (jnp.sqrt(accum) + EPSILON)
+            weights_out[at : at + width] = weights_ref[at : at + width] - rate
+            accum_out[:, at : at + width] = accum.T[:1]
+
+    return pl.pallas_call(
+        kernel,
+        out_shape=[
+            jax.ShapeDtypeStruct(weights_in.shape, weights_in.dtype),
+            jax.ShapeDtypeStruct(accum_in.shape, accum_in.dtype),
+        ],
+        in_specs=[SMEM] + vmem_specs(4),
+        out_specs=vmem_specs(2),
+        compiler_params=PARAMS,
+        name="update",
+    )(core[None], own, other, weights_in, accum_in)
 
 
 def pairs(shift):
@@ -191,7 +214,7 @@
     by_table, half, oth = relayout(src, rows, local)
     got = {HALF: move(half, over_z(HALF))}
     sib = move(oth, other_core)
-    rows = (rows, sib[-1, 0, : rows.shape[0]].astype(jnp.int32))
+    ids = jnp.concatenate([tile, rows, sib[-1, 0, : rows.shape[0]].astype(jnp.int32)])
 
     def both(i, j):
         return [(0, None, i * X + j), (1, (i - 1) * X + j)]
@@ -225,20 +248,19 @@
     for i in NEAR[::-1]:
         blocks = move(made[NEAR.index(i)], over_z(i))
         last.append((blocks, [(i, j, s) for s in range(2) for j in range(X)]))
-    partial = add_tiles(None, groups, tile, mult, rows, row_blocks)
-    return add_tiles(partial, last, tile, mult, rows, row_blocks)
+    partial = add_tiles(None, groups, ids, mult, row_blocks)
+    return add_tiles(partial, last, ids, mult, row_blocks)
 
 
 def on_device(pooled_grads, table, state, tile_mult, tile_rows):
     weights_in = table[0]
-    accum_in = state[0]
     mult = tile_mult[0, 0]
     rows, width = weights_in.shape
     row_blocks = rows // mult.shape[-1]
     partial_grad = exchange_and_add(pooled_grads[0, 0], mult, tile_rows[0, 0], row_blocks)
-    total_grad = sum_over_replicas(partial_grad.reshape(rows, width))
-    weights_out, accum_out = adagrad(weights_in, accum_in, total_grad)
-    return (weights_out[None], accum_out[None])
+    core, own, other = sum_over_replicas(partial_grad.reshape(rows, width))
+    weights_out, accum_out = update(core, own, other, weights_in, state)
+    return (weights_out[None], accum_out)
 
 
 def solution(mesh):

time: 164 us -> 163 us (level)
  no operation moved by 1% of the time
where the time goes in v5:
time: 163 us; the launch traced here: 160 us
  starting transfers between devices  100 us (61%)
  waiting for transfers between devices  38.5 us (24%)
  blocking collectives  12.6 us (8%)
  Pallas kernels  7.45 us (5%)
    ppermute x16, starting transfers between devices, move(): return lax.ppermute(value, ('mp', 'replica'), pairs(shift))  93.8 us
    ppermute x16, waiting for transfers between devices, move(): return lax.ppermute(value, ('mp', 'replica'), pairs(shift))  36.4 us
    all_to_all x1, blocking collectives, sum_over_replicas(): lax.all_to_all(copies, 'replica', split_axis=0, concat_axis=0, axis_index...  12.6 us
    ppermute x1, starting transfers between devices, sum_over_replicas(): other = lax.ppermute(own, 'replica', swap)  3.71 us
  transfers between devices with their start and end apart: 18, of which 7 were waited for; matrix products, arithmetic and copies ran while one was open for 0% of the time, Pallas kernels for 3%

profile of v5, /device:TPU:1, one launch (start us, length us, event | category | flops | bytes accessed | tf_op | source)
XLA Modules:
  0.0 160.2 jit_solution(10288346370270334815)
XLA Ops:
  0.6 8.7 %collective-permute-start.1 = (bf16[64,128,128]{2,1,0:T(8,128)(2,1)}, bf16[64,128,128]{2,1,0:T(8,128)(2,1)S(1)}, u32[]{:S(2)}, u32[]{:S(2)}) collective-permute-start(bf16[64,128,128]{2,1,0:T(8,128)(2,1)} %bitcast.17), channel_id=1, source_target_pairs={{0,1},{1,0},{2,3},{3,2},{4,5},{5,4},{6,7},{7,6},{8,9},{9,8},{10,11... | collective-permute-start | bytes 6291464 | tf_op jit(solution)/shard_map/ppermute | solution.py:189
  9.4 2.4 %relayout.1 = (bf16[64,128,128]{2,1,0:T(8,128)(2,1)S(1)}, bf16[4,128,128]{2,1,0:T(8,128)(2,1)S(1)}, bf16[29,128,128]{2,1,0:T(8,128)(2,1)S(1)}) custom-call(s32[64]{0:T(128)S(1)} %fusion.1.src_ref, s32[1,64]{1,0:T(1,128)} %bitcast.24, bf16[128,64,128]{2,1,0:T(8,128)(2,1)} %bitcast.22), custom_call_target="tpu_custom_call" | custom-call | tf_op jit(solution)/shard_map/relayout/pallas_call | solution.py:57
  11.9 1.9 %collective-permute-start = (bf16[29,128,128]{2,1,0:T(8,128)(2,1)S(1)}, bf16[29,128,128]{2,1,0:T(8,128)(2,1)S(1)}, u32[]{:S(2)}, u32[]{:S(2)}) collective-permute-start(bf16[29,128,128]{2,1,0:T(8,128)(2,1)S(1)} %get-tuple-element.22), channel_id=1, source_target_pairs={{0,1},{1,0},{2,3},{3,2},{4,5},{5,4},{6,7},{7,6},{8,9},{9,8},{10,11... | collective-permute-start | bytes 2850824 | tf_op jit(solution)/shard_map/ppermute | solution.py:189
  13.8 2.5 %collective-permute-done.refs_1_ = bf16[29,128,128]{2,1,0:T(8,128)(2,1)S(1)} collective-permute-done((bf16[29,128,128]{2,1,0:T(8,128)(2,1)S(1)}, bf16[29,128,128]{2,1,0:T(8,128)(2,1)S(1)}, u32[]{:S(2)}, u32[]{:S(2)}) %collective-permute-start) | collective-permute-done | bytes 950304 | tf_op jit(solution)/shard_map/ppermute | solution.py:189
  16.3 0.7 regroup.3
  17.0 9.7 %collective-permute-start.10 = (bf16[8,128,128]{2,1,0:T(8,128)(2,1)S(1)}, bf16[8,128,128]{2,1,0:T(8,128)(2,1)S(1)}, u32[]{:S(2)}, u32[]{:S(2)}) collective-permute-start(bf16[8,128,128]{2,1,0:T(8,128)(2,1)S(1)} %get-tuple-element.33), channel_id=1, source_target_pairs={{0,56},{1,73},{2,58},{3,75},{4,60},{5,77},{6,62},{7,79},{8,64},{9,... | collective-permute-start | bytes 786440 | tf_op jit(solution)/shard_map/ppermute | solution.py:189
  26.6 1.9 %collective-permute-start.11 = (bf16[8,128,128]{2,1,0:T(8,128)(2,1)S(1)}, bf16[8,128,128]{2,1,0:T(8,128)(2,1)S(1)}, u32[]{:S(2)}, u32[]{:S(2)}) collective-permute-start(bf16[8,128,128]{2,1,0:T(8,128)(2,1)S(1)} %get-tuple-element.34), channel_id=1, source_target_pairs={{0,48},{1,81},{2,50},{3,83},{4,52},{5,85},{6,54},{7,87},{8,56},{9,... | collective-permute-start | bytes 786440 | tf_op jit(solution)/shard_map/ppermute | solution.py:189
  28.6 8.6 %collective-permute-start.12 = (bf16[8,128,128]{2,1,0:T(8,128)(2,1)S(1)}, bf16[8,128,128]{2,1,0:T(8,128)(2,1)S(1)}, u32[]{:S(2)}, u32[]{:S(2)}) collective-permute-start(bf16[8,128,128]{2,1,0:T(8,128)(2,1)S(1)} %get-tuple-element.35), channel_id=1, source_target_pairs={{0,40},{1,89},{2,42},{3,91},{4,44},{5,93},{6,46},{7,95},{8,48},{9,... | collective-permute-start | bytes 786440 | tf_op jit(solution)/shard_map/ppermute | solution.py:189
  37.2 5.2 %collective-permute-start.9 = (bf16[4,128,128]{2,1,0:T(8,128)(2,1)S(1)}, bf16[4,128,128]{2,1,0:T(8,128)(2,1)S(1)}, u32[]{:S(2)}, u32[]{:S(2)}) collective-permute-start(bf16[4,128,128]{2,1,0:T(8,128)(2,1)S(1)} %get-tuple-element.32), channel_id=1, source_target_pairs={{0,64},{1,65},{2,66},{3,67},{4,68},{5,69},{6,70},{7,71},{8,72},{9,... | collective-permute-start | bytes 393224 | tf_op jit(solution)/shard_map/ppermute | solution.py:189
  42.4 25.8 %collective-permute-done.9.refs_0_ = bf16[4,128,128]{2,1,0:T(8,128)(2,1)S(1)} collective-permute-done((bf16[4,128,128]{2,1,0:T(8,128)(2,1)S(1)}, bf16[4,128,128]{2,1,0:T(8,128)(2,1)S(1)}, u32[]{:S(2)}, u32[]{:S(2)}) %collective-permute-start.9) | collective-permute-done | bytes 131104 | tf_op jit(solution)/shard_map/ppermute | solution.py:189
  68.2 2.4 %collective-permute-start.2 = (bf16[9,128,128]{2,1,0:T(8,128)(2,1)S(1)}, bf16[9,128,128]{2,1,0:T(8,128)(2,1)S(1)}, u32[]{:S(2)}, u32[]{:S(2)}) collective-permute-start(bf16[9,128,128]{2,1,0:T(8,128)(2,1)S(1)} %get-tuple-element.25), channel_id=1, source_target_pairs={{0,128},{1,129},{2,130},{3,131},{4,132},{5,133},{6,134},{7,135},{8... | collective-permute-start | bytes 884744 | tf_op jit(solution)/shard_map/ppermute | solution.py:189
  70.5 0.0 collective-permute-done.10.refs_1_
  70.6 4.4 %collective-permute-start.3 = (bf16[9,128,128]{2,1,0:T(8,128)(2,1)S(1)}, bf16[9,128,128]{2,1,0:T(8,128)(2,1)S(1)}, u32[]{:S(2)}, u32[]{:S(2)}) collective-permute-start(bf16[9,128,128]{2,1,0:T(8,128)(2,1)S(1)} %get-tuple-element.26), channel_id=1, source_target_pairs={{0,256},{1,257},{2,258},{3,259},{4,260},{5,261},{6,262},{7,263},{8... | collective-permute-start | bytes 884744 | tf_op jit(solution)/shard_map/ppermute | solution.py:189
  74.9 0.0 collective-permute-done.11.refs_2_
  74.9 0.0 copy-start.3
  74.9 0.0 copy-start
  75.0 10.7 %collective-permute-start.4 = (bf16[9,128,128]{2,1,0:T(8,128)(2,1)S(1)}, bf16[9,128,128]{2,1,0:T(8,128)(2,1)S(1)}, u32[]{:S(2)}, u32[]{:S(2)}) collective-permute-start(bf16[9,128,128]{2,1,0:T(8,128)(2,1)S(1)} %get-tuple-element.27), channel_id=1, source_target_pairs={{0,384},{1,385},{2,386},{3,387},{4,388},{5,389},{6,390},{7,391},{8... | collective-permute-start | bytes 884744 | tf_op jit(solution)/shard_map/ppermute | solution.py:189
  85.7 0.0 collective-permute-done.12.refs_3_
  85.7 0.0 collective-permute-done.1.refs_4_.mult1
  85.7 0.6 regroup.5
  86.3 6.5 %collective-permute-start.13 = (bf16[7,128,128]{2,1,0:T(8,128)(2,1)S(1)}, bf16[7,128,128]{2,1,0:T(8,128)(2,1)S(1)}, u32[]{:S(2)}, u32[]{:S(2)}) collective-permute-start(bf16[7,128,128]{2,1,0:T(8,128)(2,1)S(1)} %get-tuple-element.37), channel_id=1, source_target_pairs={{0,128},{1,129},{2,130},{3,131},{4,132},{5,133},{6,134},{7,135},{8... | collective-permute-start | bytes 688136 | tf_op jit(solution)/shard_map/ppermute | solution.py:189
  92.8 4.4 %collective-permute-start.14 = (bf16[7,128,128]{2,1,0:T(8,128)(2,1)S(1)}, bf16[7,128,128]{2,1,0:T(8,128)(2,1)S(1)}, u32[]{:S(2)}, u32[]{:S(2)}) collective-permute-start(bf16[7,128,128]{2,1,0:T(8,128)(2,1)S(1)} %get-tuple-element.38), channel_id=1, source_target_pairs={{0,256},{1,257},{2,258},{3,259},{4,260},{5,261},{6,262},{7,263},{8... | collective-permute-start | bytes 688136 | tf_op jit(solution)/shard_map/ppermute | solution.py:189
  97.2 0.0 collective-permute-done.2.refs_1_
  97.2 0.0 collective-permute-done.3.refs_2_
  97.2 0.0 collective-permute-done.4.refs_3_
  97.2 0.6 regroup.4
  97.8 4.1 %collective-permute-start.5 = (bf16[8,128,128]{2,1,0:T(8,128)(2,1)S(1)}, bf16[8,128,128]{2,1,0:T(8,128)(2,1)S(1)}, u32[]{:S(2)}, u32[]{:S(2)}) collective-permute-start(bf16[8,128,128]{2,1,0:T(8,128)(2,1)S(1)} %get-tuple-element.28), channel_id=1, source_target_pairs={{0,32},{1,97},{2,34},{3,99},{4,36},{5,101},{6,38},{7,103},{8,40},{... | collective-permute-start | bytes 786440 | tf_op jit(solution)/shard_map/ppermute | solution.py:189
  102.0 17.3 %collective-permute-start.6 = (bf16[8,128,128]{2,1,0:T(8,128)(2,1)S(1)}, bf16[8,128,128]{2,1,0:T(8,128)(2,1)S(1)}, u32[]{:S(2)}, u32[]{:S(2)}) collective-permute-start(bf16[8,128,128]{2,1,0:T(8,128)(2,1)S(1)} %get-tuple-element.29), channel_id=1, source_target_pairs={{0,24},{1,105},{2,26},{3,107},{4,28},{5,109},{6,30},{7,111},{8,32}... | collective-permute-start | bytes 786440 | tf_op jit(solution)/shard_map/ppermute | solution.py:189
  119.2 1.9 %collective-permute-start.7 = (bf16[8,128,128]{2,1,0:T(8,128)(2,1)S(1)}, bf16[8,128,128]{2,1,0:T(8,128)(2,1)S(1)}, u32[]{:S(2)}, u32[]{:S(2)}) collective-permute-start(bf16[8,128,128]{2,1,0:T(8,128)(2,1)S(1)} %get-tuple-element.30), channel_id=1, source_target_pairs={{0,16},{1,113},{2,18},{3,115},{4,20},{5,117},{6,22},{7,119},{8,24}... | collective-permute-start | bytes 786440 | tf_op jit(solution)/shard_map/ppermute | solution.py:189
  121.2 0.0 collective-permute-done.13.refs_5_
  121.2 2.2 %collective-permute-start.8 = (bf16[8,128,128]{2,1,0:T(8,128)(2,1)S(1)}, bf16[8,128,128]{2,1,0:T(8,128)(2,1)S(1)}, u32[]{:S(2)}, u32[]{:S(2)}) collective-permute-start(bf16[8,128,128]{2,1,0:T(8,128)(2,1)S(1)} %get-tuple-element.31), channel_id=1, source_target_pairs={{0,8},{1,121},{2,10},{3,123},{4,12},{5,125},{6,14},{7,127},{8,16},... | collective-permute-start | bytes 786440 | tf_op jit(solution)/shard_map/ppermute | solution.py:189
  123.4 0.0 collective-permute-done.14.refs_6_
  123.4 4.0 %collective-permute-start.15 = (bf16[7,128,128]{2,1,0:T(8,128)(2,1)S(1)}, bf16[7,128,128]{2,1,0:T(8,128)(2,1)S(1)}, u32[]{:S(2)}, u32[]{:S(2)}) collective-permute-start(bf16[7,128,128]{2,1,0:T(8,128)(2,1)S(1)} %get-tuple-element.39), channel_id=1, source_target_pairs={{0,384},{1,385},{2,386},{3,387},{4,388},{5,389},{6,390},{7,391},{8... | collective-permute-start | bytes 688136 | tf_op jit(solution)/shard_map/ppermute | solution.py:189
  127.4 0.1 pad_add_fusion.ids_ref
  127.5 3.0 %collective-permute-done.15.refs_7_ = bf16[7,128,128]{2,1,0:T(8,128)(2,1)S(1)} collective-permute-done((bf16[7,128,128]{2,1,0:T(8,128)(2,1)S(1)}, bf16[7,128,128]{2,1,0:T(8,128)(2,1)S(1)}, u32[]{:S(2)}, u32[]{:S(2)}) %collective-permute-start.15) | collective-permute-done | bytes 229408 | tf_op jit(solution)/shard_map/ppermute | solution.py:189
  130.5 1.1 add_tiles.2.refs_4_
  131.5 0.0 collective-permute-done.5.refs_0_
  131.5 2.4 %collective-permute-done.7.refs_2_ = bf16[8,128,128]{2,1,0:T(8,128)(2,1)S(1)} collective-permute-done((bf16[8,128,128]{2,1,0:T(8,128)(2,1)S(1)}, bf16[8,128,128]{2,1,0:T(8,128)(2,1)S(1)}, u32[]{:S(2)}, u32[]{:S(2)}) %collective-permute-start.7) | collective-permute-done | bytes 262176 | tf_op jit(solution)/shard_map/ppermute | solution.py:189
  133.9 2.8 %collective-permute-done.8.refs_3_ = bf16[8,128,128]{2,1,0:T(8,128)(2,1)S(1)} collective-permute-done((bf16[8,128,128]{2,1,0:T(8,128)(2,1)S(1)}, bf16[8,128,128]{2,1,0:T(8,128)(2,1)S(1)}, u32[]{:S(2)}, u32[]{:S(2)}) %collective-permute-start.8) | collective-permute-done | bytes 262176 | tf_op jit(solution)/shard_map/ppermute | solution.py:189
  136.7 1.1 add_tiles.3
  137.8 0.0 copy-start.1
  137.8 0.0 copy-start.2
  137.8 2.9 %collective-permute-start.16 = (f32[512,128]{1,0:T(8,128)S(1)}, f32[512,128]{1,0:T(8,128)S(1)}, u32[]{:S(2)}, u32[]{:S(2)}) collective-permute-start(f32[512,128]{1,0:T(8,128)S(1)} %bitcast.20), channel_id=1, source_target_pairs={{0,1},{1,0},{2,3},{3,2},{4,5},{5,4},{6,7},{7,6},{8,9},{9,8},{10,11... | collective-permute-start | bytes 786440 | tf_op jit(solution)/shard_map/ppermute | solution.py:132
  140.7 1.1 collective-permute-done.16
  141.9 12.6 %all_to_all.5 = f32[4,256,128]{2,1,0:T(8,128)S(1)} all-to-all(f32[4,256,128]{2,1,0:T(8,128)S(1)} %broadcast_in_dim.16), channel_id=1, replica_groups={{0,2,4,6},{1,3,5,7},{8,10,12,14},{9,11,13,15},{16,18,20,22},{17,19,21,2..., dimensions={0} | all-to-all | bytes 1048576 | tf_op jit(solution)/shard_map/all_to_all | solution.py:137
  154.5 3.7 %collective-permute-start.17 = (f32[256,128]{1,0:T(8,128)S(1)}, f32[256,128]{1,0:T(8,128)S(1)}, u32[]{:S(2)}, u32[]{:S(2)}) collective-permute-start(f32[256,128]{1,0:T(8,128)S(1)} %reduce_sum.9.own_ref), channel_id=1, source_target_pairs={{0,1},{1,0},{2,3},{3,2},{4,5},{5,4},{6,7},{7,6},{8,9},{9,8},{10,11... | collective-permute-start | bytes 393224 | tf_op jit(solution)/shard_map/ppermute | solution.py:141
  158.2 1.0 collective-permute-done.17.other_ref
  159.2 1.0 update.1
  (12 shorter events, 0.2 us)
Async XLA Ops:
  0.6 85.1 %collective-permute-start.1 = (bf16[64,128,128]{2,1,0:T(8,128)(2,1)}, bf16[64,128,128]{2,1,0:T(8,128)(2,1)S(1)}, u32[]{:S(2)}, u32[]{:S(2)}) collective-permute-start(bf16[64,128,128]{2,1,0:T(8,128)(2,1)} %bitcast.17), channel_id=1, source_target_pairs={{0,1},{1,0},{2,3},{3,2},{4,5},{5,4},{6,7},{7,6},{8,9},{9,8},{10,11... | collective-permute-start | bytes 6291464 | tf_op jit(solution)/shard_map/ppermute | solution.py:189
  11.9 4.4 %collective-permute-start = (bf16[29,128,128]{2,1,0:T(8,128)(2,1)S(1)}, bf16[29,128,128]{2,1,0:T(8,128)(2,1)S(1)}, u32[]{:S(2)}, u32[]{:S(2)}) collective-permute-start(bf16[29,128,128]{2,1,0:T(8,128)(2,1)S(1)} %get-tuple-element.22), channel_id=1, source_target_pairs={{0,1},{1,0},{2,3},{3,2},{4,5},{5,4},{6,7},{7,6},{8,9},{9,8},{10,11... | collective-permute-start | bytes 2850824 | tf_op jit(solution)/shard_map/ppermute | solution.py:189
  17.0 53.6 %collective-permute-start.10 = (bf16[8,128,128]{2,1,0:T(8,128)(2,1)S(1)}, bf16[8,128,128]{2,1,0:T(8,128)(2,1)S(1)}, u32[]{:S(2)}, u32[]{:S(2)}) collective-permute-start(bf16[8,128,128]{2,1,0:T(8,128)(2,1)S(1)} %get-tuple-element.33), channel_id=1, source_target_pairs={{0,56},{1,73},{2,58},{3,75},{4,60},{5,77},{6,62},{7,79},{8,64},{9,... | collective-permute-start | bytes 786440 | tf_op jit(solution)/shard_map/ppermute | solution.py:189
  26.6 48.3 %collective-permute-start.11 = (bf16[8,128,128]{2,1,0:T(8,128)(2,1)S(1)}, bf16[8,128,128]{2,1,0:T(8,128)(2,1)S(1)}, u32[]{:S(2)}, u32[]{:S(2)}) collective-permute-start(bf16[8,128,128]{2,1,0:T(8,128)(2,1)S(1)} %get-tuple-element.34), channel_id=1, source_target_pairs={{0,48},{1,81},{2,50},{3,83},{4,52},{5,85},{6,54},{7,87},{8,56},{9,... | collective-permute-start | bytes 786440 | tf_op jit(solution)/shard_map/ppermute | solution.py:189
  28.6 57.1 %collective-permute-start.12 = (bf16[8,128,128]{2,1,0:T(8,128)(2,1)S(1)}, bf16[8,128,128]{2,1,0:T(8,128)(2,1)S(1)}, u32[]{:S(2)}, u32[]{:S(2)}) collective-permute-start(bf16[8,128,128]{2,1,0:T(8,128)(2,1)S(1)} %get-tuple-element.35), channel_id=1, source_target_pairs={{0,40},{1,89},{2,42},{3,91},{4,44},{5,93},{6,46},{7,95},{8,48},{9,... | collective-permute-start | bytes 786440 | tf_op jit(solution)/shard_map/ppermute | solution.py:189
  37.2 30.9 %collective-permute-start.9 = (bf16[4,128,128]{2,1,0:T(8,128)(2,1)S(1)}, bf16[4,128,128]{2,1,0:T(8,128)(2,1)S(1)}, u32[]{:S(2)}, u32[]{:S(2)}) collective-permute-start(bf16[4,128,128]{2,1,0:T(8,128)(2,1)S(1)} %get-tuple-element.32), channel_id=1, source_target_pairs={{0,64},{1,65},{2,66},{3,67},{4,68},{5,69},{6,70},{7,71},{8,72},{9,... | collective-permute-start | bytes 393224 | tf_op jit(solution)/shard_map/ppermute | solution.py:189
  68.2 29.0 %collective-permute-start.2 = (bf16[9,128,128]{2,1,0:T(8,128)(2,1)S(1)}, bf16[9,128,128]{2,1,0:T(8,128)(2,1)S(1)}, u32[]{:S(2)}, u32[]{:S(2)}) collective-permute-start(bf16[9,128,128]{2,1,0:T(8,128)(2,1)S(1)} %get-tuple-element.25), channel_id=1, source_target_pairs={{0,128},{1,129},{2,130},{3,131},{4,132},{5,133},{6,134},{7,135},{8... | collective-permute-start | bytes 884744 | tf_op jit(solution)/shard_map/ppermute | solution.py:189
  70.6 26.6 %collective-permute-start.3 = (bf16[9,128,128]{2,1,0:T(8,128)(2,1)S(1)}, bf16[9,128,128]{2,1,0:T(8,128)(2,1)S(1)}, u32[]{:S(2)}, u32[]{:S(2)}) collective-permute-start(bf16[9,128,128]{2,1,0:T(8,128)(2,1)S(1)} %get-tuple-element.26), channel_id=1, source_target_pairs={{0,256},{1,257},{2,258},{3,259},{4,260},{5,261},{6,262},{7,263},{8... | collective-permute-start | bytes 884744 | tf_op jit(solution)/shard_map/ppermute | solution.py:189
  74.9 52.4 %copy-start.3 = (s32[1,1,64]{2,1,0:T(1,128)S(1)}, s32[1,1,64]{2,1,0:T(1,128)}, u32[]{:S(2)}) copy-start(s32[1,1,64]{2,1,0:T(1,128)} %param.9) | copy-start | bytes 772
  74.9 55.5 %copy-start = (bf16[1,1,64,128,128]{4,3,2,1,0:T(8,128)(2,1)S(1)}, bf16[1,1,64,128,128]{4,3,2,1,0:T(8,128)(2,1)}, u32[]{:S(2)}) copy-start(bf16[1,1,64,128,128]{4,3,2,1,0:T(8,128)(2,1)} %param.8) | copy-start | bytes 6291460
  75.0 22.3 %collective-permute-start.4 = (bf16[9,128,128]{2,1,0:T(8,128)(2,1)S(1)}, bf16[9,128,128]{2,1,0:T(8,128)(2,1)S(1)}, u32[]{:S(2)}, u32[]{:S(2)}) collective-permute-start(bf16[9,128,128]{2,1,0:T(8,128)(2,1)S(1)} %get-tuple-element.27), channel_id=1, source_target_pairs={{0,384},{1,385},{2,386},{3,387},{4,388},{5,389},{6,390},{7,391},{8... | collective-permute-start | bytes 884744 | tf_op jit(solution)/shard_map/ppermute | solution.py:189
  86.3 34.9 %collective-permute-start.13 = (bf16[7,128,128]{2,1,0:T(8,128)(2,1)S(1)}, bf16[7,128,128]{2,1,0:T(8,128)(2,1)S(1)}, u32[]{:S(2)}, u32[]{:S(2)}) collective-permute-start(bf16[7,128,128]{2,1,0:T(8,128)(2,1)S(1)} %get-tuple-element.37), channel_id=1, source_target_pairs={{0,128},{1,129},{2,130},{3,131},{4,132},{5,133},{6,134},{7,135},{8... | collective-permute-start | bytes 688136 | tf_op jit(solution)/shard_map/ppermute | solution.py:189
  92.8 30.6 %collective-permute-start.14 = (bf16[7,128,128]{2,1,0:T(8,128)(2,1)S(1)}, bf16[7,128,128]{2,1,0:T(8,128)(2,1)S(1)}, u32[]{:S(2)}, u32[]{:S(2)}) collective-permute-start(bf16[7,128,128]{2,1,0:T(8,128)(2,1)S(1)} %get-tuple-element.38), channel_id=1, source_target_pairs={{0,256},{1,257},{2,258},{3,259},{4,260},{5,261},{6,262},{7,263},{8... | collective-permute-start | bytes 688136 | tf_op jit(solution)/shard_map/ppermute | solution.py:189
  97.8 33.7 %collective-permute-start.5 = (bf16[8,128,128]{2,1,0:T(8,128)(2,1)S(1)}, bf16[8,128,128]{2,1,0:T(8,128)(2,1)S(1)}, u32[]{:S(2)}, u32[]{:S(2)}) collective-permute-start(bf16[8,128,128]{2,1,0:T(8,128)(2,1)S(1)} %get-tuple-element.28), channel_id=1, source_target_pairs={{0,32},{1,97},{2,34},{3,99},{4,36},{5,101},{6,38},{7,103},{8,40},{... | collective-permute-start | bytes 786440 | tf_op jit(solution)/shard_map/ppermute | solution.py:189
  102.0 29.5 %collective-permute-start.6 = (bf16[8,128,128]{2,1,0:T(8,128)(2,1)S(1)}, bf16[8,128,128]{2,1,0:T(8,128)(2,1)S(1)}, u32[]{:S(2)}, u32[]{:S(2)}) collective-permute-start(bf16[8,128,128]{2,1,0:T(8,128)(2,1)S(1)} %get-tuple-element.29), channel_id=1, source_target_pairs={{0,24},{1,105},{2,26},{3,107},{4,28},{5,109},{6,30},{7,111},{8,32}... | collective-permute-start | bytes 786440 | tf_op jit(solution)/shard_map/ppermute | solution.py:189
  119.2 14.6 %collective-permute-start.7 = (bf16[8,128,128]{2,1,0:T(8,128)(2,1)S(1)}, bf16[8,128,128]{2,1,0:T(8,128)(2,1)S(1)}, u32[]{:S(2)}, u32[]{:S(2)}) collective-permute-start(bf16[8,128,128]{2,1,0:T(8,128)(2,1)S(1)} %get-tuple-element.30), channel_id=1, source_target_pairs={{0,16},{1,113},{2,18},{3,115},{4,20},{5,117},{6,22},{7,119},{8,24}... | collective-permute-start | bytes 786440 | tf_op jit(solution)/shard_map/ppermute | solution.py:189
  121.2 15.5 %collective-permute-start.8 = (bf16[8,128,128]{2,1,0:T(8,128)(2,1)S(1)}, bf16[8,128,128]{2,1,0:T(8,128)(2,1)S(1)}, u32[]{:S(2)}, u32[]{:S(2)}) collective-permute-start(bf16[8,128,128]{2,1,0:T(8,128)(2,1)S(1)} %get-tuple-element.31), channel_id=1, source_target_pairs={{0,8},{1,121},{2,10},{3,123},{4,12},{5,125},{6,14},{7,127},{8,16},... | collective-permute-start | bytes 786440 | tf_op jit(solution)/shard_map/ppermute | solution.py:189
  123.4 7.1 %collective-permute-start.15 = (bf16[7,128,128]{2,1,0:T(8,128)(2,1)S(1)}, bf16[7,128,128]{2,1,0:T(8,128)(2,1)S(1)}, u32[]{:S(2)}, u32[]{:S(2)}) collective-permute-start(bf16[7,128,128]{2,1,0:T(8,128)(2,1)S(1)} %get-tuple-element.39), channel_id=1, source_target_pairs={{0,384},{1,385},{2,386},{3,387},{4,388},{5,389},{6,390},{7,391},{8... | collective-permute-start | bytes 688136 | tf_op jit(solution)/shard_map/ppermute | solution.py:189
  137.8 21.4 %copy-start.1 = (f32[1,512,128]{2,1,0:T(8,128)S(1)}, f32[1,512,128]{2,1,0:T(8,128)}, u32[]{:S(2)}) copy-start(f32[1,512,128]{2,1,0:T(8,128)} %param.6) | copy-start | bytes 786436
  137.8 21.4 %copy-start.2 = (f32[1,512]{1,0:T(1,128)S(1)}, f32[1,512]{1,0:T(1,128)}, u32[]{:S(2)}) copy-start(f32[1,512]{1,0:T(1,128)} %accum_ref.1) | copy-start | bytes 6148
  137.8 4.0 %collective-permute-start.16 = (f32[512,128]{1,0:T(8,128)S(1)}, f32[512,128]{1,0:T(8,128)S(1)}, u32[]{:S(2)}, u32[]{:S(2)}) collective-permute-start(f32[512,128]{1,0:T(8,128)S(1)} %bitcast.20), channel_id=1, source_target_pairs={{0,1},{1,0},{2,3},{3,2},{4,5},{5,4},{6,7},{7,6},{8,9},{9,8},{10,11... | collective-permute-start | bytes 786440 | tf_op jit(solution)/shard_map/ppermute | solution.py:132
  154.5 4.7 %collective-permute-start.17 = (f32[256,128]{1,0:T(8,128)S(1)}, f32[256,128]{1,0:T(8,128)S(1)}, u32[]{:S(2)}, u32[]{:S(2)}) collective-permute-start(f32[256,128]{1,0:T(8,128)S(1)} %reduce_sum.9.own_ref), channel_id=1, source_target_pairs={{0,1},{1,0},{2,3},{3,2},{4,5},{5,4},{6,7},{7,6},{8,9},{9,8},{10,11... | collective-permute-start | bytes 393224 | tf_op jit(solution)/shard_map/ppermute | solution.py:141
